TPU v7x, 512 devices: a whole 4x8x8 slice. The times are simulated.
512 devices in a mesh: tm: 32 (over z, x), lm: 16 (over y, core).
Axes of the slice: x: 4, y: 8, z: 8, core: 2. Of those that a mesh axis runs over, the one named last changes fastest.
Arguments:
- camera_poses: float32 [6, 32768], P(None, 'tm'), may hold values from -1.5 to 1.5
- landmarks: float32 [3, 262144], P(None, ('tm', 'lm')), may hold values from -5 to 5
- odometry: float32 [6, 32768], P(None, 'tm'), may hold values from -1.5 to 1.5
- odometry_info: float32 [32768], P('tm'), may hold values from 100 to 3000
- observations: bfloat16 [49152, 3, 64, 64], P(('tm', 'lm')), may hold values from -6 to 6
- tile_frame: int32 [49152], P(('tm', 'lm')), may hold values from 0 to 15, as said below
- tile_block: int32 [49152], P(('tm', 'lm')), may hold values from 0 to 127, as said below
- tile_count: int32 [512], P(('tm', 'lm')), may hold values from 38 to 96, as said below
- block_slot: int32 [32, 128], P('tm'), may hold values from 0 to 127, each once within a row
Outputs:
- refined_poses: float32 [6, 32768], P(None, 'tm')
- refined_points: float32 [3, 262144], P(None, ('tm', 'lm'))
Inputs may be any that keep to these rules, and one draw needn't show every extreme that they name: `tile_frame`: frame blocks of the slot's own time shard. `tile_block`: landmark block ids of the slot's own time shard. `tile_count`: slots from this count on hold no live tile; some device is full. `block_slot`: each row is a permutation of the 128 block ids.
All inputs are finite; a program needn't handle non-finite values.
Results may differ from a plain program's by a relative error of at most 0.0003.
Values sent between devices are 32-bit elements; how exact they have to be, the bound alone decides.
No kernel may reach another device: no remote copies, remote signals or barrier semaphores. Data moves between devices by JAX's collectives and lax.ppermute only.
A program may use at most 64 MiB of HBM per device.

v0:
```python
import jax
import jax.numpy as jnp
from jax import lax
from jax.sharding import PartitionSpec as P

TILE = 64
ITERS = 2


robust_scale = 4.0
damping = 1.0
moment_pairs = ((0, 0), (1, 1), (2, 2), (0, 1), (0, 2), (1, 2))


def extended_2(array, sides, width):
    for axis, dim in sides:
        count, length = (lax.axis_size(axis), array.shape[dim])
        up = [(i, (i + 1) % count) for i in range(count - 1)]
        down = [(j, i) for i, j in up]
        last = lax.slice_in_dim(array, length - width, length, axis=dim)
        initial = lax.slice_in_dim(array, 0, width, axis=dim)
        before = lax.ppermute(last, axis, up)
        after = lax.ppermute(initial, axis, down)
        array = jnp.concatenate([before, array, after], axis=dim)
    return array


def cross_product(left, right):
    return [
        left[1] * right[2] - left[2] * right[1],
        left[2] * right[0] - left[0] * right[2],
        left[0] * right[1] - left[1] * right[0],
    ]


def tile_terms(rotation, offset, points, measured_tiles, live_mask):
    rotation_rows = [rotation[k][:, :, None] for k in range(3)]
    offset_rows = [offset[k][:, :, None] for k in range(3)]
    point_columns = [points[k][:, None, :] for k in range(3)]
    measured = measured_tiles.astype(jnp.float32)
    turned = cross_product(rotation_rows, point_columns)
    residual = [point_columns[k] + turned[k] + offset_rows[k] - measured[:, k] for k in range(3)]
    squared = residual[0] * residual[0] + residual[1] * residual[1] + residual[2] * residual[2]
    weight = live_mask[:, None, None] / (1.0 + squared / robust_scale)
    weighted = [weight * residual[k] for k in range(3)]
    lever = cross_product(point_columns, weighted)
    frame_terms = [jnp.sum(lever[k], axis=2) for k in range(3)]
    frame_terms += [jnp.sum(weighted[k], axis=2) for k in range(3)]
    frame_terms += [jnp.sum(weight, axis=2)]
    frame_terms += [jnp.sum(weight * point_columns[k], axis=2) for k in range(3)]
    frame_terms += [
        jnp.sum(weight * (point_columns[a] * point_columns[b]), axis=2) for a, b in moment_pairs
    ]
    spun = cross_product(rotation_rows, weighted)
    point_terms = [jnp.sum(weighted[k] - spun[k], axis=1) for k in range(3)]
    rotation_square = (
        rotation_rows[0] * rotation_rows[0]
        + rotation_rows[1] * rotation_rows[1]
        + rotation_rows[2] * rotation_rows[2]
    )
    point_terms += [jnp.sum(weight * (1.0 + rotation_square), axis=1)]
    point_terms += [
        jnp.sum(weight * (rotation_rows[a] * rotation_rows[b]), axis=1) for a, b in moment_pairs
    ]
    return (jnp.stack(frame_terms, axis=1), jnp.stack(point_terms, axis=1))


def block_solve(matrix, vector):
    dimension = len(vector)
    factor = [[None] * dimension for i in range(dimension)]
    inverse_diag = [None] * dimension
    for i in range(dimension):
        for j in range(i + 1):
            running = matrix[i][j]
            for k in range(j):
                running = running - factor[i][k] * factor[j][k]
            if i == j:
                factor[i][i] = jnp.sqrt(running)
                inverse_diag[i] = 1.0 / factor[i][i]
            else:
                factor[i][j] = running * inverse_diag[j]
    forward = [None] * dimension
    for i in range(dimension):
        running = vector[i]
        for k in range(i):
            running = running - factor[i][k] * forward[k]
        forward[i] = running * inverse_diag[i]
    solution = [None] * dimension
    for i in reversed(range(dimension)):
        running = forward[i]
        for k in range(i + 1, dimension):
            running = running - factor[k][i] * solution[k]
        solution[i] = running * inverse_diag[i]
    return solution


def pose_step(sums, current, link_grad, link_diag):
    moments = [sums[10 + m] for m in range(6)]
    centroid = [sums[7 + m] for m in range(3)]
    counted = sums[6]
    diagonal_add = link_diag + damping
    zero_entry = jnp.zeros_like(counted)
    rotation_block = [
        [moments[1] + moments[2] + diagonal_add, -moments[3], -moments[4]],
        [-moments[3], moments[0] + moments[2] + diagonal_add, -moments[5]],
        [-moments[4], -moments[5], moments[0] + moments[1] + diagonal_add],
    ]
    cross_block = [
        [zero_entry, -centroid[2], centroid[1]],
        [centroid[2], zero_entry, -centroid[0]],
        [-centroid[1], centroid[0], zero_entry],
    ]
    matrix = []
    for i in range(3):
        matrix.append(rotation_block[i] + cross_block[i])
    for i in range(3):
        offset_row = [counted + diagonal_add if i == k else zero_entry for k in range(3)]
        matrix.append([cross_block[k][i] for k in range(3)] + offset_row)
    gradient = [sums[k] + link_grad[k] for k in range(6)]
    solution = block_solve(matrix, gradient)
    return current - jnp.stack(solution)


def point_step(sums, current):
    diagonal = sums[3] + damping
    outer = [sums[4 + m] for m in range(6)]
    matrix = [
        [diagonal - outer[0], -outer[3], -outer[4]],
        [-outer[3], diagonal - outer[1], -outer[5]],
        [-outer[4], -outer[5], diagonal - outer[2]],
    ]
    solution = block_solve(matrix, [sums[0], sums[1], sums[2]])
    return current - jnp.stack(solution)


def fetch_window(owned_points):
    return lax.all_gather(owned_points, "lm", axis=1, tiled=True)


def on_device(
    camera_poses,
    landmarks,
    odometry,
    odometry_info,
    observations,
    tile_frame,
    tile_block,
    tile_count,
    block_slot,
):
    frames = camera_poses.shape[1]
    blocks = frames // TILE
    tile_slots = observations.shape[0]
    owner_count = lax.axis_size("lm")
    own_points = landmarks.shape[1]
    window_blocks = own_points * owner_count // TILE
    live_mask = (jnp.arange(tile_slots) < tile_count[0]).astype(jnp.float32)
    positions = jnp.sum(
        jnp.where(
            tile_block[:, None] == jnp.arange(window_blocks)[None, :], block_slot[0][None, :], 0
        ),
        axis=1,
    )
    frame_onehot = (tile_frame[:, None] == jnp.arange(blocks)[None, :]).astype(jnp.float32)
    point_onehot = (positions[:, None] == jnp.arange(window_blocks)[None, :]).astype(jnp.float32)
    final_frame = (lax.axis_index("tm") == lax.axis_size("tm") - 1) & (
        jnp.arange(frames) == frames - 1
    )
    link_rows = jnp.concatenate([odometry, odometry_info[None, :]], axis=0)
    window = None
    for iteration in range(ITERS):
        window = fetch_window(landmarks)
        pose_blocks = camera_poses.reshape(6, blocks, TILE)
        picked = jnp.take(pose_blocks, tile_frame, axis=1)
        seen_points = jnp.take(window.reshape(3, window_blocks, TILE), positions, axis=1)
        frame_part, point_part = tile_terms(
            picked[0:3], picked[3:6], seen_points, observations, live_mask
        )
        frame_local = jnp.einsum(
            "tf,tqi->qfi", frame_onehot, frame_part, precision=lax.Precision.HIGHEST
        ).reshape(16, frames)
        point_local = jnp.einsum(
            "tp,tqi->qpi", point_onehot, point_part, precision=lax.Precision.HIGHEST
        ).reshape(10, window_blocks * TILE)
        extended = extended_2(jnp.concatenate([camera_poses, link_rows], axis=0), (("tm", 1),), 1)
        following = extended[0:6, 2:]
        previous = extended[0:6, :-2]
        motion_before = extended[6:12, :-2]
        weight_before = extended[12, :-2]
        weight_after = jnp.where(final_frame, 0.0, odometry_info)
        ahead_gap = following - camera_poses - odometry
        behind_gap = camera_poses - previous - motion_before
        link_grad = -weight_after[None, :] * ahead_gap + weight_before[None, :] * behind_gap
        link_diag = weight_after + weight_before
        frame_totals = lax.psum(frame_local, "lm")
        next_poses = pose_step(frame_totals, camera_poses, link_grad, link_diag)
        owned_sums = lax.psum_scatter(point_local, "lm", scatter_dimension=1, tiled=True)
        landmarks = point_step(owned_sums, landmarks)
        window = None
        camera_poses = next_poses
    return (camera_poses, landmarks)


def solution(mesh):
    return jax.shard_map(
        on_device,
        mesh=mesh,
        in_specs=(
            P(None, "tm"),
            P(None, ("tm", "lm")),
            P(None, "tm"),
            P("tm"),
            P(("tm", "lm"), None, None, None),
            P(("tm", "lm")),
            P(("tm", "lm")),
            P(("tm", "lm")),
            P("tm", None),
        ),
        out_specs=(P(None, "tm"), P(None, ("tm", "lm"))),
        check_vma=False,
    )
```

profile of v0, /device:TPU:1, one launch (start us, length us, event | category | flops | bytes accessed | tf_op | source)
XLA Modules:
  0.0 448.4 jit_solution(16103786936685141534)
XLA Ops:
  7.2 0.9 select_reduce_fusion
  9.4 21.5 %all_gather.6 = f32[3,8192]{1,0:T(4,128)S(1)} all-gather(f32[3,512]{1,0:T(4,128)} %param.14), channel_id=1, replica_groups=mesh['tm'=32,'lm'=16] {'lm'}, dimensions={1}, use_global_device_ids=true | all-gather | bytes 104448 | tf_op jit(solution)/shard_map/all_gather | solution.py:137
  33.3 1.4 gather_fusion.1
  34.7 1.2 select_bitcast_fusion
  35.9 0.9 fusion.68
  36.9 0.8 add_add_fusion.1
  37.8 0.9 copy.173
  38.7 0.9 copy.174
  39.6 1.5 copy.175
  41.1 1.5 copy.176
  42.5 1.5 copy.177
  44.0 1.5 copy.178
  45.5 1.5 copy.179
  47.0 1.5 copy.180
  48.5 1.5 copy.181
  50.0 1.5 copy.182
  51.4 1.5 copy.183
  52.9 1.5 copy.184
  54.4 1.5 copy.185
  55.9 0.9 copy.169
  56.8 0.9 copy.171
  57.6 0.9 copy.172
  58.7 0.7 convert_element_type.14
  60.2 6.6 %multiply_reduce_fusion.16 = (f32[96,64]{0,1:T(8,128)S(1)}, f32[96,64]{0,1:T(8,128)S(1)}, f32[96,64]{0,1:T(8,128)S(1)}, f32[96,64]{0,1:T(8,128)S(1)}, f32[96,64]...) fusion(f32[96,64]{0,1:T(8,128)S(1)} %copy-done.15, ...), kind=kLoop, calls=%fused_computation.33 | loop fusion | flops 23095296 | bytes 7250304 | tf_op jit(solution)/shard_map/reduce_sum | solution.py:63
  66.8 1.9 fusion.1
  68.7 3.8 subtract_reduce_fusion.6
  74.4 1.3 collective-permute-start.1
  75.7 1.3 collective-permute-start
  77.8 1.0 reshape.351
  79.1 1.0 collective-permute-done
  80.2 100.0 %all-reduce.3.cloned.1.call-done = f32[16,1024]{1,0:T(8,128)} async-done(((f32[16,1024]{1,0:T(8,128)}), f32[16,1024]{1,0:T(8,128)}) %all-reduce.3.cloned.1.call-update) | async-done | bytes 65552 | tf_op jit(solution)/shard_map/psum | solution.py:195
  180.3 1.1 slice_add_fusion.17
  181.3 1.0 slice_add_fusion.11
  184.7 2.9 collective-permute-start.3
  187.6 1.3 collective-permute-start.2
  189.1 3.0 collective-permute-done.2
  192.1 47.6 %reduce-scatter.3.cloned.1.call-done = f32[10,512]{1,0:T(8,128)} async-done(((f32[10,8192]{1,0:T(8,128)}), f32[10,512]{1,0:T(8,128)}) %reduce-scatter.3.cloned.1.call-update) | async-done | bytes 20496 | tf_op jit(solution)/shard_map/reduce_scatter | solution.py:197
  239.8 1.1 subtract_multiply_fusion.34
  240.8 16.7 %all_gather.7 = f32[3,8192]{1,0:T(4,128)S(1)} all-gather(f32[3,512]{1,0:T(4,128)S(1)} %maximum_subtract_fusion), channel_id=1, replica_groups=mesh['tm'=32,'lm'=16] {'lm'}, dimensions={1}, use_global_device_ids=true | all-gather | bytes 104448 | tf_op jit(solution)/shard_map/all_gather | solution.py:137
  259.7 8.2 %multiply_reduce_fusion = (f32[96,64]{0,1:T(8,128)S(1)}, f32[96,64]{0,1:T(8,128)S(1)}, f32[96,64]{0,1:T(8,128)S(1)}, f32[96,64]{0,1:T(8,128)S(1)}, f32[96,64]{0,...) fusion(f32[96,64]{0,1:T(8,128)S(1)} %copy.213, ...), kind=kLoop, calls=%fused_computation.7 | loop fusion | flops 23095296 | bytes 7250304 | tf_op jit(solution)/shard_map/reduce_sum | solution.py:63
  268.0 1.9 fusion.4
  269.8 3.8 subtract_reduce_fusion
  276.2 1.0 reshape.355
  277.2 103.6 %all-reduce.5.cloned.1.call-done = f32[16,1024]{1,0:T(8,128)} async-done(((f32[16,1024]{1,0:T(8,128)}), f32[16,1024]{1,0:T(8,128)}) %all-reduce.5.cloned.1.call-update) | async-done | bytes 65552 | tf_op jit(solution)/shard_map/psum | solution.py:195
  380.8 1.0 slice_add_fusion.5
  381.8 1.1 slice_add_fusion.14
  383.8 56.4 %reduce-scatter.5.cloned.1.call-done = f32[10,512]{1,0:T(8,128)} async-done(((f32[10,8192]{1,0:T(8,128)}), f32[10,512]{1,0:T(8,128)}) %reduce-scatter.5.cloned.1.call-update) | async-done | bytes 20496 | tf_op jit(solution)/shard_map/reduce_scatter | solution.py:197
  440.2 1.1 subtract_multiply_fusion.32
  (196 shorter events, 14.9 us)
Async XLA Ops:
  7.2 26.0 %copy-start.3 = (f32[6,1024]{1,0:T(8,128)S(1)}, f32[6,1024]{1,0:T(8,128)}, u32[]{:S(2)}) copy-start(f32[6,1024]{1,0:T(8,128)} %param.13) | copy-start | bytes 73732
  7.2 173.1 %all-reduce.3.cloned.1.call-start = ((), (), s32[]{:S(2)}) async-start(), calls=%async_computation.2 | async-start | bytes 131072 | tf_op jit(solution)/shard_map/psum | solution.py:195
  8.1 24.1 %copy-start.20 = (s32[96]{0:T(128)}, s32[96]{0:T(128)S(1)}, u32[]{:S(2)}) copy-start(s32[96]{0:T(128)S(1)} %select_reduce_fusion) | copy-start | bytes 1156
  9.4 25.3 %copy-start.17 = (pred[96]{0:T(512)(128)(4,1)}, pred[96]{0:T(512)(128)(4,1)S(1)}, u32[]{:S(2)}) copy-start(pred[96]{0:T(512)(128)(4,1)S(1)} %compare_and_fusion) | copy-start | bytes 292
  33.3 25.2 %copy-start.1 = (bf16[96,3,64,64]{0,3,2,1:T(8,128)(2,1)S(1)}, bf16[96,3,64,64]{0,3,2,1:T(8,128)(2,1)}, u32[]{:S(2)}) copy-start(bf16[96,3,64,64]{0,3,2,1:T(8,128)(2,1)} %param.17) | copy-start | bytes 7077892
  58.5 1.5 copy-start.5
  58.5 1.5 copy-start.6
  58.6 1.5 copy-start.7
  58.6 1.5 copy-start.8
  58.6 1.5 copy-start.9
  58.6 1.5 copy-start.10
  58.6 1.5 copy-start.11
  58.6 1.5 copy-start.12
  58.6 1.5 copy-start.13
  58.6 1.5 copy-start.14
  58.6 1.5 copy-start.15
  59.4 7.4 %copy-start = (f32[96,3,64,64]{0,3,2,1:T(8,128)}, f32[96,3,64,64]{0,3,2,1:T(8,128)S(1)}, u32[]{:S(2)}) copy-start(f32[96,3,64,64]{0,3,2,1:T(8,128)S(1)} %convert_element_type.14) | copy-start | bytes 14155780
  68.7 4.1 copy-start.19
  68.7 5.6 %copy-start.2 = (f32[6,1024]{1,0:T(8,128)S(1)}, f32[6,1024]{1,0:T(8,128)}, u32[]{:S(2)}) copy-start(f32[6,1024]{1,0:T(8,128)} %param.15) | copy-start | bytes 73732
  68.7 5.6 %copy-start.4 = (f32[1024]{0:T(1024)S(1)}, f32[1024]{0:T(1024)}, u32[]{:S(2)}) copy-start(f32[1024]{0:T(1024)} %param.16) | copy-start | bytes 12292
  72.6 4.6 %copy-start.21 = (s32[96]{0:T(128)S(1)}, s32[96]{0:T(128)}, u32[]{:S(2)}) copy-start(s32[96]{0:T(128)} %copy-done.20) | copy-start | bytes 1156
  74.3 165.5 %reduce-scatter.3.cloned.1.call-start = ((), (), s32[]{:S(2)}) async-start(), calls=%async_computation.3 | async-start | bytes 557056 | tf_op jit(solution)/shard_map/reduce_scatter | solution.py:197
  74.4 4.5 collective-permute-start.1
  75.7 4.4 collective-permute-start
  77.5 105.8 %copy-start.18 = (pred[96]{0:T(512)(128)(4,1)S(1)}, pred[96]{0:T(512)(128)(4,1)}, u32[]{:S(2)}) copy-start(pred[96]{0:T(512)(128)(4,1)} %copy-done.17) | copy-start | bytes 292
  78.9 302.0 %all-reduce.5.cloned.1.call-start = ((), (), s32[]{:S(2)}) async-start(), calls=%async_computation.4 | async-start | bytes 131072 | tf_op jit(solution)/shard_map/psum | solution.py:195
  182.6 58.2 %copy-start.16 = (f32[3,512]{1,0:T(4,128)S(1)}, f32[3,512]{1,0:T(4,128)}, u32[]{:S(2)}) copy-start(f32[3,512]{1,0:T(4,128)} %param.14) | copy-start | bytes 18436
  184.7 4.2 collective-permute-start.3
  187.6 4.4 collective-permute-start.2
  258.6 9.3 %slice-start = ((s8[6291456]{0:T(1024)(128)(4,1)}), s8[2097152]{0:T(1024)(128)(4,1)S(1)}, s32[]{:S(2)}) async-start(s8[6291456]{0:T(1024)(128)(4,1)} %bitcast.290), calls=%async_computation.6 | async-start | bytes 4194304
  259.7 8.3 %slice-start.1 = ((s8[6291456]{0:T(1024)(128)(4,1)}), s8[4194304]{0:T(1024)(128)(4,1)S(1)}, s32[]{:S(2)}) async-start(s8[6291456]{0:T(1024)(128)(4,1)} %bitcast.290), calls=%async_computation.7 | async-start | bytes 8388608
  275.4 164.8 %reduce-scatter.5.cloned.1.call-start = ((), (), s32[]{:S(2)}) async-start(), calls=%async_computation.5 | async-start | bytes 557056 | tf_op jit(solution)/shard_map/reduce_scatter | solution.py:197
Sparse Core Ops, SparseCore 0:
  74.4 105.8 all-reduce.2
  183.0 56.6 reduce-scatter.2
  275.5 105.2 all-reduce.4
  383.5 56.6 reduce-scatter.4
where the time goes:
time: 451 us; the launch traced here: 448 us
  waiting for transfers between devices  312 us (69%)
  other arithmetic  40.7 us (9%)
  blocking collectives  38.2 us (8%)
  local copies, waits for them, and re-layouts  33 us (7%)
  between operations  15.6 us (3%)
  starting transfers between devices  6.92 us (2%)
    psum x2, waiting for transfers between devices, on_device(): frame_totals = lax.psum(frame_local, 'lm')  204 us
    reduce_scatter x2, waiting for transfers between devices, on_device(): lax.psum_scatter(point_local, 'lm', scatter_dimension=1, tiled=True)  104 us
    all_gather x2, blocking collectives, fetch_window(): return lax.all_gather(owned_points, 'lm', axis=1, tiled=True)  38.2 us
    reduce_sum x2, other arithmetic, tile_terms(): jnp.sum(weight * (rotation_rows[a] * rotation_rows[b]), axis=1)  14.9 us
  transfers between devices with their start and end apart: 8, of which 6 were waited for; matrix products, arithmetic and copies ran while one was open for 2% of the time, Pallas kernels for 0%

commit v1 on v0

v1 whole, which is shorter than its diff:
```python
import jax
import jax.numpy as jnp
from jax import lax
from jax.experimental import pallas as pl
from jax.experimental.pallas import tpu as pltpu
from jax.sharding import PartitionSpec as P

TILE = 64
ITERS = 2
damping = 1.0
scale = 4.0


def vmem():
    return pl.BlockSpec(memory_space=pltpu.VMEM)


def lanes(shape):
    return lax.broadcasted_iota(jnp.int32, shape, 1)


def half_turn(x):
    return pltpu.roll(x, 64, 1)


def own_block(ref, block):
    pair = jnp.zeros((8, 128), jnp.float32)
    for h in range(8):
        pair = jnp.where(block // 2 == h, ref[:, h * 128 : (h + 1) * 128], pair)
    return jnp.where(block % 2 == 1, half_turn(pair), pair)


def pack_kernel(points_ref, poses_ref, odometry_ref, info_ref, copies_ref, edge_ref, link_ref, rows, chunk):
    owner = lax.axis_index("lm")
    lane = lanes((8, 128))
    rows[...] = jnp.zeros((8, 1024), jnp.float32)
    rows[0:6, :] = odometry_ref[...]
    rows[6:7, :] = info_ref[...]
    current = own_block(rows, owner)
    before = own_block(rows, owner - 1)
    link_ref[:, 0:128] = current
    link_ref[:, 128:256] = jnp.where(lane == 0, pltpu.roll(before, 65, 1), pltpu.roll(current, 1, 1))
    rows[...] = jnp.zeros((8, 1024), jnp.float32)
    rows[0:6, :] = poses_ref[...]
    pose = own_block(rows, owner)
    edge_ref[:, 0:128] = pose
    edge_ref[:, 128:256] = current
    for k in range(3):
        for b in range(8):
            chunk[b : b + 1, k * 64 : (k + 1) * 64] = points_ref[k : k + 1, b * 64 : (b + 1) * 64]
    chunk[:, 192:256] = half_turn(pose)[:, 64:128]
    whole = chunk[...]
    for d in range(copies_ref.shape[0]):
        copies_ref[d] = whole


def split(x, parts):
    pieces = []
    for _ in range(parts - 1):
        pieces.append(x.astype(jnp.bfloat16))
        x = x - pieces[-1].astype(jnp.float32)
    pieces.append(x.astype(jnp.bfloat16))
    return pieces


def dot(a, b):
    return lax.dot_general(a, b, (((1,), (0,)), ((), ())), preferred_element_type=jnp.float32)


def dot_t(a, b):
    return lax.dot_general(a, b, (((1,), (1,)), ((), ())), preferred_element_type=jnp.float32)


def tiles_kernel(count_ref, window_ref, seen_ref, frame_ref, block_ref, slot_ref, out_ref, pose, point, fsum, psum):
    slots = frame_ref.shape[1]
    row = lax.broadcasted_iota(jnp.int32, (128, slots), 0)
    frame = frame_ref[...]
    named = jnp.where(block_ref[...] == row, 1.0, 0.0).astype(jnp.bfloat16)
    table = jnp.broadcast_to(slot_ref[...].astype(jnp.float32), (8, 128)).astype(jnp.bfloat16)
    position = dot(table, named)[0:1].astype(jnp.int32)
    held = position == row
    live = lanes((1, slots)) < count_ref[0]
    pick = jnp.where(held, 1.0, 0.0).astype(jnp.bfloat16)
    turned = jnp.transpose(window_ref[...].reshape(128, 256), (1, 0))
    pieces = split(turned, 3)
    point[...] = sum(dot(piece[0:192], pick) for piece in pieces)
    for k in range(6):
        pick = jnp.where(frame * 8 + k == row, 1.0, 0.0).astype(jnp.bfloat16)
        pose[k * 64 : (k + 1) * 64, :] = sum(dot(piece[192:256], pick) for piece in pieces)
    psum[...] = jnp.zeros_like(psum)

    def step(i, carry):
        w = [jnp.broadcast_to(pose[pl.ds(k * 64 + i, 1), :], (8, slots)) for k in range(3)]
        t = [jnp.broadcast_to(pose[pl.ds(192 + k * 64 + i, 1), :], (8, slots)) for k in range(3)]
        w00, w11, w22 = w[0] * w[0], w[1] * w[1], w[2] * w[2]
        m00, m11, m22 = 1.0 + (w11 + w22), 1.0 + (w00 + w22), 1.0 + (w00 + w11)
        m01, m02, m12 = w[0] * w[1], w[0] * w[2], w[1] * w[2]
        total = [None] * 16
        for g in range(4):
            seen = [seen_ref[k, i, g * 16 : (g + 1) * 16, :].astype(jnp.float32) for k in range(3)]
            for h in range(2):
                at = g * 16 + h * 8
                x = [point[k * 64 + at : k * 64 + at + 8, :] for k in range(3)]
                o = [seen[k][h * 8 : (h + 1) * 8] for k in range(3)]
                r0 = (x[0] + t[0] - o[0]) + (w[1] * x[2] - w[2] * x[1])
                r1 = (x[1] + t[1] - o[1]) + (w[2] * x[0] - w[0] * x[2])
                r2 = (x[2] + t[2] - o[2]) + (w[0] * x[1] - w[1] * x[0])
                c = 1.0 / (scale + (r0 * r0 + r1 * r1 + r2 * r2))
                c0, c1, c2 = c * r0, c * r1, c * r2
                y = [c * x[k] for k in range(3)]
                terms = [
                    x[1] * c2 - x[2] * c1,
                    x[2] * c0 - x[0] * c2,
                    x[0] * c1 - x[1] * c0,
                    c0,
                    c1,
                    c2,
                    c,
                    y[0],
                    y[1],
                    y[2],
                    y[0] * x[0],
                    y[1] * x[1],
                    y[2] * x[2],
                    y[0] * x[1],
                    y[0] * x[2],
                    y[1] * x[2],
                ]
                total = terms if total[0] is None else [p + q for p, q in zip(total, terms)]
                terms = [
                    c * m00,
                    c * m11,
                    c * m22,
                    c * m01,
                    c * m02,
                    c * m12,
                    c0 - (w[1] * c2 - w[2] * c1),
                    c1 - (w[2] * c0 - w[0] * c2),
                    c2 - (w[0] * c1 - w[1] * c0),
                ]
                for q, term in enumerate(terms):
                    psum[q * 64 + at : q * 64 + at + 8, :] += term
        for q in range(16):
            fsum[pl.ds(q * 64 + i, 1), :] = jnp.sum(total[q], axis=0, keepdims=True)
        return carry

    lax.fori_loop(0, 64, step, 0)
    weight = jnp.where(live, scale, 0.0)
    own = jnp.where(frame == lax.broadcasted_iota(jnp.int32, (16, slots), 0), weight, 0.0).astype(jnp.bfloat16)
    frames = sum(dot_t(own, piece) for piece in split(fsum[...], 3))
    for r in range(8):
        out_ref[:, 40 + r, :] = frames[:, r * 128 : (r + 1) * 128]
    own = jnp.where(held, weight, 0.0).astype(jnp.bfloat16)
    for q in range(5):
        wide = 128 if q < 4 else 64
        part = sum(dot_t(own, piece) for piece in split(psum[q * 128 : q * 128 + wide, :], 3))
        if wide < 128:
            part = jnp.concatenate([part, jnp.zeros_like(part)], axis=1)
        out_ref[:, q * 8 : (q + 1) * 8, :] = part.reshape(16, 8, 128)


def solve3(m00, m11, m22, m01, m02, m12, b0, b1, b2):
    i0 = 1.0 / m00
    l1, l2 = m01 * i0, m02 * i0
    d1 = m11 - l1 * m01
    e = m12 - l1 * m02
    i1 = 1.0 / d1
    l3 = e * i1
    d2 = m22 - l2 * m02 - l3 * e
    y1 = b1 - l1 * b0
    y2 = b2 - l2 * b0 - l3 * y1
    x2 = y2 / d2
    x1 = y1 * i1 - l3 * x2
    x0 = b0 * i0 - l1 * x1 - l2 * x2
    return x0, x1, x2


def new_poses(sums, window_ref, link_ref, edge_ref, first_edge_ref, scratch):
    owner, shard = lax.axis_index("lm"), lax.axis_index("tm")
    owners, shards = lax.axis_size("lm"), lax.axis_size("tm")
    lane = lanes((8, 128))
    current = half_turn(window_ref[owner, :, 128:256])
    before = half_turn(window_ref[jnp.maximum(owner - 1, 0), :, 128:256])
    after = half_turn(window_ref[jnp.minimum(owner + 1, owners - 1), :, 128:256])
    outside = edge_ref[:, 0:128]
    initial, final = owner == 0, owner == owners - 1
    before = jnp.where(initial, outside, before)
    after = jnp.where(final, outside, after)
    previous = jnp.where(lane == 0, pltpu.roll(before, 65, 1), pltpu.roll(current, 1, 1))
    following = jnp.where(lane == 63, pltpu.roll(after, 63, 1), pltpu.roll(current, 127, 1))
    motion = link_ref[:, 0:128]
    motion_before = link_ref[:, 128:256]
    outside = pltpu.roll(first_edge_ref[:, 128:256], 65, 1)
    motion_before = jnp.where((lane == 0) & initial, outside, motion_before)
    ends = (lane[0:1] == 63) & final & (shard == shards - 1)
    starts = (lane[0:1] == 0) & initial & (shard == 0)
    weight_after = jnp.where(ends, 0.0, motion[6:7])
    weight_before = jnp.where(starts, 0.0, motion_before[6:7])
    scratch[0:8] = weight_before * (current - previous - motion_before) - weight_after * (
        following - current - motion
    )
    scratch[8:16] = sums
    scratch[16:24] = half_turn(sums)
    f = [scratch[8 + 8 * (q % 2) + q // 2 : 9 + 8 * (q % 2) + q // 2, :] for q in range(16)]
    g = [f[k] + scratch[k : k + 1, :] for k in range(6)]
    diagonal = weight_after + weight_before + damping
    s, c, m = f[6] + diagonal, f[7:10], f[10:16]
    inverse = 1.0 / s
    d = [c[k] * inverse for k in range(3)]
    n00 = m[1] + m[2] + diagonal - (c[1] * d[1] + c[2] * d[2])
    n11 = m[0] + m[2] + diagonal - (c[0] * d[0] + c[2] * d[2])
    n22 = m[0] + m[1] + diagonal - (c[0] * d[0] + c[1] * d[1])
    n01, n02, n12 = c[0] * d[1] - m[3], c[0] * d[2] - m[4], c[1] * d[2] - m[5]
    b0 = g[0] - (d[1] * g[5] - d[2] * g[4])
    b1 = g[1] - (d[2] * g[3] - d[0] * g[5])
    b2 = g[2] - (d[0] * g[4] - d[1] * g[3])
    x0, x1, x2 = solve3(n00, n11, n22, n01, n02, n12, b0, b1, b2)
    x3 = (g[3] + (c[1] * x2 - c[2] * x1)) * inverse
    x4 = (g[4] + (c[2] * x0 - c[0] * x2)) * inverse
    x5 = (g[5] + (c[0] * x1 - c[1] * x0)) * inverse
    for k, x in enumerate((x0, x1, x2, x3, x4, x5)):
        scratch[k : k + 1, :] = x
    return current - scratch[0:8]


def new_points(sums_ref, window_ref):
    owner = lax.axis_index("lm")
    owned = window_ref[owner]
    x = [owned[:, 0:128], half_turn(owned[:, 0:128]), owned[:, 128:256]]
    q = []
    for k in range(5):
        pair = sums_ref[0, k * 8 : (k + 1) * 8, :]
        for d in range(1, sums_ref.shape[0]):
            pair = pair + sums_ref[d, k * 8 : (k + 1) * 8, :]
        q += [pair, half_turn(pair)]
    moved = solve3(q[0] + damping, q[1] + damping, q[2] + damping, -q[3], -q[4], -q[5], q[6], q[7], q[8])
    return [x[k] - moved[k] for k in range(3)]


def frame_sums(sums_ref):
    total = sums_ref[0, 40:48, :]
    for d in range(1, sums_ref.shape[0]):
        total = total + sums_ref[d, 40:48, :]
    return total


def update_kernel(sums_ref, window_ref, link_ref, edge_ref, copies_ref, sent_ref, scratch):
    lower = lanes((8, 128)) < 64
    pose = new_poses(frame_sums(sums_ref), window_ref, link_ref, edge_ref, edge_ref, scratch)
    sent_ref[...] = pose
    x = new_points(sums_ref, window_ref)
    left = jnp.where(lower, x[0], half_turn(x[1]))
    right = jnp.where(lower, x[2], half_turn(pose))
    for d in range(copies_ref.shape[0]):
        copies_ref[d, :, 0:128] = left
        copies_ref[d, :, 128:256] = right


def last_poses_kernel(sums_ref, window_ref, link_ref, edge_ref, first_edge_ref, copies_ref, scratch):
    pose = new_poses(frame_sums(sums_ref), window_ref, link_ref, edge_ref, first_edge_ref, scratch)
    for d in range(copies_ref.shape[0]):
        copies_ref[d] = pose


def last_points_kernel(sums_ref, window_ref, out_ref):
    x = new_points(sums_ref, window_ref)
    for k in range(3):
        for b in range(8):
            out_ref[k : k + 1, b * 64 : (b + 1) * 64] = x[k][b : b + 1, 0:64]


def spread_kernel(poses_ref, out_ref):
    lower = lanes((8, 128)) < 64
    for h in range(8):
        pair = jnp.where(lower, poses_ref[2 * h], half_turn(poses_ref[2 * h + 1]))
        out_ref[:, h * 128 : (h + 1) * 128] = pair[0:6]


def call(kernel, outs, scratch, *args, smem=0):
    specs = [pl.BlockSpec(memory_space=pltpu.SMEM)] * smem + [vmem()] * (len(args) - smem)
    single = not isinstance(outs, (list, tuple))
    return pl.pallas_call(
        kernel,
        out_shape=outs,
        in_specs=specs,
        out_specs=vmem() if single else [vmem()] * len(outs),
        scratch_shapes=scratch,
        compiler_params=pltpu.CompilerParams(vmem_limit_bytes=24 << 20),
    )(*args)


def exchange(array):
    return lax.all_to_all(array, "lm", 0, 0, tiled=True)


def on_device(
    camera_poses,
    landmarks,
    odometry,
    odometry_info,
    observations,
    tile_frame,
    tile_block,
    tile_count,
    block_slot,
):
    owners, shards = lax.axis_size("lm"), lax.axis_size("tm")
    slots = observations.shape[0]
    f32 = jnp.float32
    seen = jnp.transpose(observations, (1, 2, 3, 0))
    to_edges = []
    for a in range(shards - 1):
        to_edges.append((a * owners + owners - 1, (a + 1) * owners))
        to_edges.append(((a + 1) * owners, a * owners + owners - 1))

    def edges(array):
        return lax.ppermute(array, ("tm", "lm"), to_edges)

    chunks = jax.ShapeDtypeStruct((owners, 8, 256), f32)
    wide = jax.ShapeDtypeStruct((8, 256), f32)
    narrow = jax.ShapeDtypeStruct((8, 128), f32)
    small = [pltpu.VMEM((24, 128), f32)]
    copies, sent, link = call(
        pack_kernel,
        [chunks, wide, wide],
        [pltpu.VMEM((8, 1024), f32), pltpu.VMEM((8, 256), f32)],
        landmarks,
        camera_poses,
        odometry,
        odometry_info[None, :],
    )
    first_edge = None
    for iteration in range(ITERS):
        window = exchange(copies)
        edge = edges(sent)
        sums = call(
            tiles_kernel,
            jax.ShapeDtypeStruct((owners, 48, 128), f32),
            [
                pltpu.VMEM((384, slots), f32),
                pltpu.VMEM((192, slots), f32),
                pltpu.VMEM((1024, slots), f32),
                pltpu.VMEM((576, slots), f32),
            ],
            tile_count,
            window,
            seen,
            tile_frame[None, :],
            tile_block[None, :],
            block_slot,
            smem=1,
        )
        sums = exchange(sums)
        if iteration == 0:
            first_edge = edge
            copies, sent = call(update_kernel, [chunks, narrow], small, sums, window, link, edge)
    copies = call(
        last_poses_kernel,
        jax.ShapeDtypeStruct((owners, 8, 128), f32),
        small,
        sums,
        window,
        link,
        edge,
        first_edge,
    )
    gathered = exchange(copies)
    points = call(last_points_kernel, jax.ShapeDtypeStruct(landmarks.shape, f32), [], sums, window)
    poses = call(spread_kernel, jax.ShapeDtypeStruct(camera_poses.shape, f32), [], gathered)
    return (poses, points)


def solution(mesh):
    return jax.shard_map(
        on_device,
        mesh=mesh,
        in_specs=(
            P(None, "tm"),
            P(None, ("tm", "lm")),
            P(None, "tm"),
            P("tm"),
            P(("tm", "lm"), None, None, None),
            P(("tm", "lm")),
            P(("tm", "lm")),
            P(("tm", "lm")),
            P("tm", None),
        ),
        out_specs=(P(None, "tm"), P(None, ("tm", "lm"))),
        check_vma=False,
    )
```

time: 451 us -> 112 us (0.25)
  waiting for transfers between devices: 312 us -> 41.8 us
  other arithmetic: 40.7 us -> 0 us
  blocking collectives: 38.2 us -> 11.8 us
  Pallas kernels: 0 us -> 22.1 us
  local copies, waits for them, and re-layouts: 33 us -> 12.4 us
  starting transfers between devices: 6.92 us -> 21.7 us
  between operations: 15.6 us -> 1.43 us
    psum x2 -> x0, waiting for transfers between devices: 204 us -> none  [on_device(): frame_totals = lax.psum(frame_local, 'lm')]
    reduce_scatter x2 -> x0, waiting for transfers between devices: 104 us -> none  [on_device(): lax.psum_scatter(point_local, 'lm', scatter_dimension=1, tiled=True)]
    all_to_all x0 -> x4, waiting for transfers between devices: none -> 41.8 us  [exchange(): return lax.all_to_all(array, 'lm', 0, 0, tiled=True)]
    all_gather x2 -> x0, blocking collectives: 38.2 us -> none  [fetch_window(): return lax.all_gather(owned_points, 'lm', axis=1, tiled=True)]
    reduce_sum x5 -> x0, other arithmetic: 23.4 us -> none  [the longest x2 14.9 us: tile_terms(): jnp.sum(weight * (rotation_rows[a] * rotation_rows[b]), axis=1)]
    pallas_call x0 -> x7, Pallas kernels: none -> 22.1 us  [call(): pl.pallas_call(kernel, out_shape=outs, in_specs=specs, out_specs=vmem() i...]
    all_to_all x0 -> x4, starting transfers between devices: none -> 20.4 us  [exchange(): return lax.all_to_all(array, 'lm', 0, 0, tiled=True)]
    mul x35 -> x0, local copies, waits for them, and re-layouts: 18.4 us -> none  [the longest x12 8.21 us: tile_terms(): point_columns[a] * point_columns[b]]
  transfers between devices with their start and end apart: 8 -> 6, of which waited for: 6 -> 4; matrix products, arithmetic and copies ran while one was open for 2% -> 0% of each run, Pallas kernels for 0% -> 1%
where the time goes in v1:
time: 112 us; the launch traced here: 111 us
  waiting for transfers between devices  41.8 us (37%)
  Pallas kernels  22.1 us (20%)
  starting transfers between devices  21.7 us (19%)
  local copies, waits for them, and re-layouts  12.4 us (11%)
  blocking collectives  11.8 us (11%)
  between operations  1.43 us (1%)
    all_to_all x4, waiting for transfers between devices, exchange(): return lax.all_to_all(array, 'lm', 0, 0, tiled=True)  41.8 us
    pallas_call x7, Pallas kernels, call(): pl.pallas_call(kernel, out_shape=outs, in_specs=specs, out_specs=vmem() i...  22.1 us
    all_to_all x4, starting transfers between devices, exchange(): return lax.all_to_all(array, 'lm', 0, 0, tiled=True)  20.4 us
    unnamed x38, local copies, waits for them, and re-layouts  12.4 us
    all_to_all x1, blocking collectives, exchange(): return lax.all_to_all(array, 'lm', 0, 0, tiled=True)  11.8 us
  transfers between devices with their start and end apart: 6, of which 4 were waited for; matrix products, arithmetic and copies ran while one was open for 0% of the time, Pallas kernels for 1%

profile of v1, /device:TPU:1, one launch (start us, length us, event | category | flops | bytes accessed | tf_op | source)
XLA Modules:
  0.0 111.2 jit_solution(16788634663119304420)
XLA Ops:
  0.6 0.0 copy-start.6
  0.6 0.7 copy-done.6
  1.4 0.0 copy-start.7
  1.4 0.8 copy-done.7
  2.1 0.0 copy-start.8
  2.1 0.7 copy-done.8
  2.8 0.0 copy-start.9
  2.8 0.7 copy-done.9
  3.5 0.8 shard_map.104
  4.4 0.0 copy-start.16
  4.4 0.6 copy-done.16
  5.0 10.1 %all-to-all-start = ((f32[16,8,256]{2,1,0:T(8,128)}), f32[16,8,256]{2,1,0:T(8,128)S(1)}, u32[]{:S(2)}, u32[]{:S(2)}) async-start(f32[16,8,256]{2,1,0:T(8,128)} %get-tuple-element.7), calls=%async_computation | async-start | bytes 262144 | tf_op jit(solution)/shard_map/all_to_all | solution.py:293
  15.7 8.5 %all-to-all-done.window_ref = f32[16,8,256]{2,1,0:T(8,128)S(1)} async-done(((f32[16,8,256]{2,1,0:T(8,128)}), f32[16,8,256]{2,1,0:T(8,128)S(1)}, u32[]{:S(2)}, u32[]{:S(2)}) %all-to-all-start) | async-done | bytes 131104 | tf_op jit(solution)/shard_map/all_to_all | solution.py:293
  24.3 0.0 copy-start.4
  24.3 1.9 %copy-done = bf16[96,3,64,64]{0,3,2,1:T(8,128)(2,1)S(1)} copy-done((bf16[96,3,64,64]{0,3,2,1:T(8,128)(2,1)S(1)}, bf16[96,3,64,64]{0,3,2,1:T(8,128)(2,1)}, u32[]{:S(2)}) %copy-start) | copy-done | bytes 2359320
  26.2 0.7 copy-done.10
  26.9 0.7 copy-done.12
  27.5 0.7 copy-done.14
  28.2 9.4 %shard_map.105 = f32[16,48,128]{2,1,0:T(8,128)S(1)} custom-call(s32[1]{0:T(128)S(6)} %copy.11.count_ref, f32[16,8,256]{2,1,0:T(8,128)S(1)} %all-to-all-done.window_ref, bf16[3,64,64,96]{3,2,1,0:T(8,128)(2,1)S(1)} %bitcast.4, s32[1,96]{1,0:T(1,128)S(1)} %bitcast.7, s32[1,96]{1,0:T(1,128)S(1)} %bitcast.9, s32[1,128]{1,0:T(1,128)S(1)} %copy-done.14), custom_call_target="tpu_custom_call" | custom-call | tf_op jit(solution)/shard_map/pallas_call | solution.py:282
  37.6 0.0 copy-start.3
  37.6 0.8 copy-done.3
  38.3 0.0 copy-done.4
  38.3 3.4 %all-to-all-start.1 = ((f32[16,48,128]{2,1,0:T(8,128)}), f32[16,48,128]{2,1,0:T(8,128)S(1)}, u32[]{:S(2)}, u32[]{:S(2)}) async-start(f32[16,48,128]{2,1,0:T(8,128)} %copy-done.3), calls=%async_computation.1 | async-start | bytes 786432 | tf_op jit(solution)/shard_map/all_to_all | solution.py:293
  41.8 0.7 collective-permute-start
  42.5 0.0 collective-permute-done.edge_ref.first_edge_ref
  42.5 13.3 %all-to-all-done.1.sums_ref = f32[16,48,128]{2,1,0:T(8,128)S(1)} async-done(((f32[16,48,128]{2,1,0:T(8,128)}), f32[16,48,128]{2,1,0:T(8,128)S(1)}, u32[]{:S(2)}, u32[]{:S(2)}) %all-to-all-start.1) | async-done | bytes 393248 | tf_op jit(solution)/shard_map/all_to_all | solution.py:293
  55.8 0.9 copy-done.5
  56.7 0.3 shard_map.106
  56.9 0.0 copy-start.17
  56.9 0.6 copy-done.17
  57.5 11.8 %all_to_all.25.window_ref = f32[16,8,256]{2,1,0:T(8,128)S(1)} all-to-all(f32[16,8,256]{2,1,0:T(8,128)S(1)} %get-tuple-element.10), channel_id=1, replica_groups=mesh['tm'=32,'lm'=16] {'lm'}, dimensions={0} | all-to-all | bytes 262144 | tf_op jit(solution)/shard_map/all_to_all | solution.py:293
  69.3 0.0 copy-done.1
  69.3 0.7 copy-done.11
  70.0 0.7 copy-done.13
  70.6 0.7 copy-done.15
  71.3 9.4 %shard_map.107 = f32[16,48,128]{2,1,0:T(8,128)S(1)} custom-call(s32[1]{0:T(128)S(6)} %copy.11.count_ref, f32[16,8,256]{2,1,0:T(8,128)S(1)} %all_to_all.25.window_ref, bf16[3,64,64,96]{3,2,1,0:T(8,128)(2,1)S(1)} %bitcast.5, s32[1,96]{1,0:T(1,128)S(1)} %bitcast.8, s32[1,96]{1,0:T(1,128)S(1)} %bitcast.10, s32[1,128]{1,0:T(1,128)S(1)} %copy-done.15), custom_call_target="tpu_custom_call" | custom-call | tf_op jit(solution)/shard_map/pallas_call | solution.py:282
  80.6 0.0 copy-start.2
  80.7 0.8 copy-done.2
  81.4 3.4 %all-to-all-start.3 = ((f32[16,48,128]{2,1,0:T(8,128)}), f32[16,48,128]{2,1,0:T(8,128)S(1)}, u32[]{:S(2)}, u32[]{:S(2)}) async-start(f32[16,48,128]{2,1,0:T(8,128)} %copy-done.2), calls=%async_computation.3 | async-start | bytes 786432 | tf_op jit(solution)/shard_map/all_to_all | solution.py:293
  84.9 0.0 copy-done.18
  84.9 0.7 collective-permute-start.1
  85.5 0.0 collective-permute-done.1.edge_ref
  85.6 13.7 %all-to-all-done.3.sums_ref = f32[16,48,128]{2,1,0:T(8,128)S(1)} async-done(((f32[16,48,128]{2,1,0:T(8,128)}), f32[16,48,128]{2,1,0:T(8,128)S(1)}, u32[]{:S(2)}, u32[]{:S(2)}) %all-to-all-start.3) | async-done | bytes 393248 | tf_op jit(solution)/shard_map/all_to_all | solution.py:293
  99.2 0.8 shard_map.108
  100.0 3.4 %all-to-all-start.4 = ((f32[16,8,128]{2,1,0:T(8,128)}), f32[16,8,128]{2,1,0:T(8,128)S(1)}, u32[]{:S(2)}, u32[]{:S(2)}) async-start(f32[16,8,128]{2,1,0:T(8,128)} %shard_map.108), calls=%async_computation.4 | async-start | bytes 131072 | tf_op jit(solution)/shard_map/all_to_all | solution.py:293
  103.4 0.8 shard_map.110
  104.2 6.3 %all-to-all-done.4.poses_ref = f32[16,8,128]{2,1,0:T(8,128)S(1)} async-done(((f32[16,8,128]{2,1,0:T(8,128)}), f32[16,8,128]{2,1,0:T(8,128)S(1)}, u32[]{:S(2)}, u32[]{:S(2)}) %all-to-all-start.4) | async-done | bytes 65568 | tf_op jit(solution)/shard_map/all_to_all | solution.py:293
  110.5 0.7 shard_map.109
  (10 shorter events, 0.0 us)
Async XLA Ops:
  0.6 0.8 copy-start.6
  1.4 0.8 copy-start.7
  2.1 0.7 copy-start.8
  2.8 0.7 copy-start.9
  4.4 0.6 copy-start.16
  5.0 19.3 %all-to-all-start = ((f32[16,8,256]{2,1,0:T(8,128)}), f32[16,8,256]{2,1,0:T(8,128)S(1)}, u32[]{:S(2)}, u32[]{:S(2)}) async-start(f32[16,8,256]{2,1,0:T(8,128)} %get-tuple-element.7), calls=%async_computation | async-start | bytes 262144 | tf_op jit(solution)/shard_map/all_to_all | solution.py:293
  24.3 14.0 %copy-start.4 = (f32[16,8,256]{2,1,0:T(8,128)}, f32[16,8,256]{2,1,0:T(8,128)S(1)}, u32[]{:S(2)}) copy-start(f32[16,8,256]{2,1,0:T(8,128)S(1)} %all-to-all-done.window_ref) | copy-start | bytes 393220
  24.3 1.9 %copy-start = (bf16[96,3,64,64]{0,3,2,1:T(8,128)(2,1)S(1)}, bf16[96,3,64,64]{0,3,2,1:T(8,128)(2,1)}, u32[]{:S(2)}) copy-start(bf16[96,3,64,64]{0,3,2,1:T(8,128)(2,1)} %param.13) | copy-start | bytes 7077892
  26.2 0.7 copy-start.10
  26.9 0.7 copy-start.12
  27.5 0.7 copy-start.14
  28.2 41.1 %copy-start.1 = (bf16[96,3,64,64]{0,3,2,1:T(8,128)(2,1)S(1)}, bf16[96,3,64,64]{0,3,2,1:T(8,128)(2,1)}, u32[]{:S(2)}) copy-start(bf16[96,3,64,64]{0,3,2,1:T(8,128)(2,1)} %param.13) | copy-start | bytes 7077892
  37.6 0.8 copy-start.3
  38.3 17.4 %all-to-all-start.1 = ((f32[16,48,128]{2,1,0:T(8,128)}), f32[16,48,128]{2,1,0:T(8,128)S(1)}, u32[]{:S(2)}, u32[]{:S(2)}) async-start(f32[16,48,128]{2,1,0:T(8,128)} %copy-done.3), calls=%async_computation.1 | async-start | bytes 786432 | tf_op jit(solution)/shard_map/all_to_all | solution.py:293
  41.8 0.7 collective-permute-start
  55.8 0.9 copy-start.5
  56.9 0.6 copy-start.17
  57.5 27.3 %copy-start.18 = (f32[8,128]{1,0:T(8,128)S(1)}, f32[8,128]{1,0:T(8,128)}, u32[]{:S(2)}) copy-start(f32[8,128]{1,0:T(8,128)} %copy-done.17) | copy-start | bytes 12292
  69.3 0.7 copy-start.11
  70.0 0.7 copy-start.13
  70.6 0.7 copy-start.15
  80.6 0.8 copy-start.2
  81.4 17.8 %all-to-all-start.3 = ((f32[16,48,128]{2,1,0:T(8,128)}), f32[16,48,128]{2,1,0:T(8,128)S(1)}, u32[]{:S(2)}, u32[]{:S(2)}) async-start(f32[16,48,128]{2,1,0:T(8,128)} %copy-done.2), calls=%async_computation.3 | async-start | bytes 786432 | tf_op jit(solution)/shard_map/all_to_all | solution.py:293
  84.9 0.7 collective-permute-start.1
  100.0 10.5 %all-to-all-start.4 = ((f32[16,8,128]{2,1,0:T(8,128)}), f32[16,8,128]{2,1,0:T(8,128)S(1)}, u32[]{:S(2)}, u32[]{:S(2)}) async-start(f32[16,8,128]{2,1,0:T(8,128)} %shard_map.108), calls=%async_computation.4 | async-start | bytes 131072 | tf_op jit(solution)/shard_map/all_to_all | solution.py:293

commit v2 on v1

v2 whole, which is shorter than its diff:
```python
import functools

import jax
import jax.numpy as jnp
from jax import lax
from jax.experimental import pallas as pl
from jax.experimental.pallas import tpu as pltpu
from jax.sharding import PartitionSpec as P

TILE = 64
ITERS = 2
SLOTS = 96
EXTRA = 128 - SLOTS
GROUPS = SLOTS // EXTRA
PLAIN = TILE * SLOTS // 128
FOLDED = TILE - PLAIN
damping = 1.0
scale = 4.0


def lanes(shape):
    return lax.broadcasted_iota(jnp.int32, shape, 1)


def half_turn(x):
    return pltpu.roll(x, 64, 1)


def own_block(ref, block):
    pair = jnp.zeros((8, 128), jnp.float32)
    for h in range(8):
        pair = jnp.where(block // 2 == h, ref[:, h * 128 : (h + 1) * 128], pair)
    return jnp.where(block % 2 == 1, half_turn(pair), pair)


def pack_kernel(
    count_ref,
    points_hbm,
    poses_hbm,
    odometry_hbm,
    info_hbm,
    frame_hbm,
    block_hbm,
    slot_hbm,
    copies_hbm,
    edge_hbm,
    link_hbm,
    names_hbm,
    more_names_hbm,
    points,
    poses,
    odometry,
    info,
    frame,
    block,
    slot,
    rows,
    chunk,
    edge,
    link_ref,
    names_ref,
    sems,
):
    loads = [
        pltpu.make_async_copy(source, target, sems.at[n])
        for n, (source, target) in enumerate(
            [
                (poses_hbm, poses),
                (points_hbm, points),
                (odometry_hbm, odometry),
                (info_hbm, info),
                (frame_hbm, frame),
                (block_hbm, block),
                (slot_hbm, slot),
            ]
        )
    ]
    for load in loads:
        load.start()
    rows[...] = jnp.zeros((8, 1024), jnp.float32)
    owner = lax.axis_index("lm")
    lane = lanes((8, 128))
    for load in loads:
        load.wait()
    rows[0:6, :] = poses[...]
    pose = own_block(rows, owner)
    for k in range(3):
        for b in range(8):
            chunk[b : b + 1, k * 64 : (k + 1) * 64] = points[k : k + 1, b * 64 : (b + 1) * 64]
    chunk[:, 192:256] = half_turn(pose)[:, 64:128]
    owners = copies_hbm.shape[0]
    sends = [pltpu.make_async_copy(chunk, copies_hbm.at[d], sems.at[10 + d]) for d in range(owners)]
    for send in sends:
        send.start()
    rows[0:6, :] = odometry[...]
    rows[6:7, :] = info[...]
    current = own_block(rows, owner)
    before = own_block(rows, owner - 1)
    edge[:, 0:128] = pose
    edge[:, 128:256] = current
    sends.append(pltpu.make_async_copy(edge, edge_hbm, sems.at[7]))
    sends[-1].start()
    link_ref[:, 0:128] = current
    link_ref[:, 128:256] = jnp.where(lane == 0, pltpu.roll(before, 65, 1), pltpu.roll(current, 1, 1))
    sends.append(pltpu.make_async_copy(link_ref, link_hbm, sems.at[8]))
    sends[-1].start()
    slots = frame.shape[1]
    row = lax.broadcasted_iota(jnp.int32, (128, slots), 0)
    named = jnp.where(block[...] == row, 1.0, 0.0).astype(jnp.bfloat16)
    table = jnp.broadcast_to(slot[...].astype(jnp.float32), (8, 128)).astype(jnp.bfloat16)
    position = dot(table, named)[0:1].astype(jnp.int32)
    live = lanes((1, slots)) < count_ref[0]
    names_ref[...] = jnp.full(names_ref.shape, -1, jnp.int32)
    names_ref[0:1, 0:slots] = jnp.where(live, frame[...], -1)
    names_ref[1:2, 0:slots] = jnp.where(live, position, -1)
    for n in range(2):
        name = names_ref[...][n : n + 1]
        for g in range(GROUPS):
            folded = jnp.where(lane[0:1] < SLOTS, name, pltpu.roll(name, SLOTS - g * EXTRA, 1))
            names_ref[2 + n * GROUPS + g : 3 + n * GROUPS + g, :] = folded
    sends.append(pltpu.make_async_copy(names_ref, names_hbm, sems.at[9]))
    sends[-1].start()
    sends.append(pltpu.make_async_copy(names_ref, more_names_hbm, sems.at[10 + owners]))
    sends[-1].start()
    for send in sends:
        send.wait()


def split(x, parts):
    pieces = []
    for _ in range(parts - 1):
        pieces.append(x.astype(jnp.bfloat16))
        x = x - pieces[-1].astype(jnp.float32)
    pieces.append(x.astype(jnp.bfloat16))
    return pieces


def dot(a, b):
    return lax.dot_general(a, b, (((1,), (0,)), ((), ())), preferred_element_type=jnp.float32)


def dot_t(a, b):
    return lax.dot_general(a, b, (((1,), (1,)), ((), ())), preferred_element_type=jnp.float32)


def fold_kernel(seen_hbm, out_hbm, seen, folded, sems):
    parts = [pl.ds(PLAIN, FOLDED)] + [pl.ds(g * FOLDED, FOLDED) for g in range(GROUPS)]
    loads = [
        pltpu.make_async_copy(seen_hbm.at[:, part], seen.at[:, part], sems.at[n]) for n, part in enumerate(parts)
    ]
    for load in loads:
        load.start()
    loads[0].wait()
    stores = []
    for g in range(GROUPS):
        loads[1 + g].wait()

        def step(m, carry):
            for k in range(3):
                for r in range(0, TILE, 16):
                    wide = seen[k, g * FOLDED + m, r : r + 16, :]
                    more = seen[k, PLAIN + m, r : r + 16, g * EXTRA : (g + 1) * EXTRA]
                    folded[k, g * FOLDED + m, r : r + 16, :] = jnp.concatenate([wide, more], axis=1)
            return carry

        lax.fori_loop(0, FOLDED, step, 0)
        part = parts[1 + g]
        stores.append(pltpu.make_async_copy(folded.at[:, part], out_hbm.at[:, part], sems.at[1 + GROUPS + g]))
        stores[-1].start()
    for store in stores:
        store.wait()


def tiles_kernel(window_ref, names_ref, seen_hbm, out_hbm, near_hbm, *scratch):
    near_ref, seen_ref, pose, point, fsum, psum, sums, sems, load_sems = scratch
    owner, owners = lax.axis_index("lm"), lax.axis_size("lm")
    chunks = load_sems.shape[0]
    pieces = PLAIN // chunks

    def load(n):
        part = pl.ds(n * pieces, pieces)
        return pltpu.make_async_copy(seen_hbm.at[:, part], seen_ref.at[:, part], load_sems.at[n])

    ahead = 2
    for n in range(ahead):
        load(n).start()
    near_ref[0] = window_ref[owner]
    near_ref[1] = window_ref[jnp.maximum(owner - 1, 0)]
    near_ref[2] = window_ref[jnp.minimum(owner + 1, owners - 1)]
    turned = split(jnp.transpose(window_ref[...].reshape(128, 256), (1, 0)), 3)
    put_near = pltpu.make_async_copy(near_ref, near_hbm, sems.at[7])
    put_near.start()
    row = lax.broadcasted_iota(jnp.int32, (128, 128), 0)
    lane = lanes((FOLDED, 128))
    points = jnp.concatenate([piece[0:192] for piece in turned], axis=0)
    for g in range(GROUPS):
        frame, position = names_ref[2 + g : 3 + g, :], names_ref[2 + GROUPS + g : 3 + GROUPS + g, :]
        pick = jnp.where(position == row, 1.0, 0.0).astype(jnp.bfloat16)
        found = dot(points, pick)
        point[g * 192 : (g + 1) * 192, :] = found[0:192] + (found[192:384] + found[384:576])
        at = 192 + g * FOLDED
        poses = jnp.concatenate(
            [piece[r : r + FOLDED] for r in (at, 192 + PLAIN) for piece in turned], axis=0
        )
        for k in range(6):
            pick = jnp.where(frame * 8 + k == row, 1.0, 0.0).astype(jnp.bfloat16)
            found = [dot(poses, pick)[n * FOLDED : (n + 1) * FOLDED] for n in range(6)]
            found = [found[n] + (found[n + 1] + found[n + 2]) for n in (0, 3)]
            pose[k * PLAIN + g * FOLDED : k * PLAIN + (g + 1) * FOLDED, :] = jnp.where(lane < SLOTS, *found)
    psum[...] = jnp.zeros_like(psum)

    def step(g, i, carry):
        w = [jnp.broadcast_to(pose[pl.ds(k * PLAIN + i, 1), :], (8, 128)) for k in range(3)]
        t = [jnp.broadcast_to(pose[pl.ds((3 + k) * PLAIN + i, 1), :], (8, 128)) for k in range(3)]
        w00, w11, w22 = w[0] * w[0], w[1] * w[1], w[2] * w[2]
        m00, m11, m22 = 1.0 + (w11 + w22), 1.0 + (w00 + w22), 1.0 + (w00 + w11)
        m01, m02, m12 = w[0] * w[1], w[0] * w[2], w[1] * w[2]
        total = [None] * 16
        for part in range(0, TILE, 16):
            seen = [seen_ref[k, i, part : part + 16, :].astype(jnp.float32) for k in range(3)]
            for h in range(2):
                at = part + h * 8
                x = [point[(g * 3 + k) * 64 + at : (g * 3 + k) * 64 + at + 8, :] for k in range(3)]
                o = [seen[k][h * 8 : (h + 1) * 8] for k in range(3)]
                r0 = (x[0] + t[0] - o[0]) + (w[1] * x[2] - w[2] * x[1])
                r1 = (x[1] + t[1] - o[1]) + (w[2] * x[0] - w[0] * x[2])
                r2 = (x[2] + t[2] - o[2]) + (w[0] * x[1] - w[1] * x[0])
                c = 1.0 / (scale + (r0 * r0 + r1 * r1 + r2 * r2))
                c0, c1, c2 = c * r0, c * r1, c * r2
                y = [c * x[k] for k in range(3)]
                terms = [
                    x[1] * c2 - x[2] * c1,
                    x[2] * c0 - x[0] * c2,
                    x[0] * c1 - x[1] * c0,
                    c0,
                    c1,
                    c2,
                    c,
                    y[0],
                    y[1],
                    y[2],
                    y[0] * x[0],
                    y[1] * x[1],
                    y[2] * x[2],
                    y[0] * x[1],
                    y[0] * x[2],
                    y[1] * x[2],
                ]
                total = terms if total[0] is None else [p + q for p, q in zip(total, terms)]
                terms = [
                    c * m00,
                    c * m11,
                    c * m22,
                    c * m01,
                    c * m02,
                    c * m12,
                    c0 - (w[1] * c2 - w[2] * c1),
                    c1 - (w[2] * c0 - w[0] * c2),
                    c2 - (w[0] * c1 - w[1] * c0),
                ]
                for q, term in enumerate(terms):
                    psum[q * 64 + at : q * 64 + at + 8, :] += term
        for q in range(16):
            fsum[pl.ds(q * 64 + i, 1), :] = jnp.sum(total[q], axis=0, keepdims=True)
        return carry

    def chunk(g, n, carry):
        load(n).wait()

        @pl.when(n + ahead < chunks)
        def _():
            load(n + ahead).start()

        return lax.fori_loop(n * pieces, (n + 1) * pieces, functools.partial(step, g), carry)

    lane = lanes((64, 128))
    each = chunks // GROUPS
    for g in range(GROUPS):
        lax.fori_loop(g * each, (g + 1) * each, functools.partial(chunk, g), 0)
        mine = (lane >= g * EXTRA) & (lane < (g + 1) * EXTRA)
        for q in range(9):
            part = psum[q * 64 : (q + 1) * 64, :]
            back = jnp.where(mine, pltpu.roll(part, (g + 1) * EXTRA, 1), 0.0)
            psum[q * 64 : (q + 1) * 64, :] = jnp.where(lane < SLOTS, part, 0.0) + back
    lane = lanes((FOLDED, 128))
    for q in range(16):
        back = jnp.zeros((FOLDED, 128), jnp.float32)
        for g in range(GROUPS):
            part = fsum[q * 64 + g * FOLDED : q * 64 + (g + 1) * FOLDED, :]
            back = jnp.where((lane >= g * EXTRA) & (lane < (g + 1) * EXTRA), pltpu.roll(part, (g + 1) * EXTRA, 1), back)
        fsum[q * 64 + PLAIN : (q + 1) * 64, :] = back
    frame, position = names_ref[0:1, :], names_ref[1:2, :]
    held = position == row
    own = jnp.where(frame == lax.broadcasted_iota(jnp.int32, (16, 128), 0), scale, 0.0).astype(jnp.bfloat16)
    frames = sum(dot_t(own, piece) for piece in split(fsum[...], 3))
    for r in range(8):
        sums[:, 40 + r, :] = frames[:, r * 128 : (r + 1) * 128]
    put_near.wait()
    stores = [pltpu.make_async_copy(sums.at[:, 40:48], out_hbm.at[:, 40:48], sems.at[5])]
    stores[0].start()
    own = jnp.where(held, scale, 0.0).astype(jnp.bfloat16)
    for q in range(5):
        wide = 128 if q < 4 else 64
        part = sum(dot_t(own, piece) for piece in split(psum[q * 128 : q * 128 + wide, :], 3))
        if wide < 128:
            part = jnp.concatenate([part, jnp.zeros_like(part)], axis=1)
        rows = slice(q * 8, (q + 1) * 8)
        sums[:, rows, :] = part.reshape(16, 8, 128)
        stores.append(pltpu.make_async_copy(sums.at[:, rows], out_hbm.at[:, rows], sems.at[q]))
        stores[-1].start()
    for store in stores:
        store.wait()


def solve3(m00, m11, m22, m01, m02, m12, b0, b1, b2):
    i0 = 1.0 / m00
    l1, l2 = m01 * i0, m02 * i0
    d1 = m11 - l1 * m01
    e = m12 - l1 * m02
    i1 = 1.0 / d1
    l3 = e * i1
    d2 = m22 - l2 * m02 - l3 * e
    y1 = b1 - l1 * b0
    y2 = b2 - l2 * b0 - l3 * y1
    x2 = y2 / d2
    x1 = y1 * i1 - l3 * x2
    x0 = b0 * i0 - l1 * x1 - l2 * x2
    return x0, x1, x2


def new_poses(sums, near_ref, link_ref, edge_ref, first_edge_ref, scratch):
    owner, shard = lax.axis_index("lm"), lax.axis_index("tm")
    owners, shards = lax.axis_size("lm"), lax.axis_size("tm")
    lane = lanes((8, 128))
    current, before, after = (half_turn(near_ref[n, :, 128:256]) for n in range(3))
    outside = edge_ref[:, 0:128]
    initial, final = owner == 0, owner == owners - 1
    before = jnp.where(initial, outside, before)
    after = jnp.where(final, outside, after)
    previous = jnp.where(lane == 0, pltpu.roll(before, 65, 1), pltpu.roll(current, 1, 1))
    following = jnp.where(lane == 63, pltpu.roll(after, 63, 1), pltpu.roll(current, 127, 1))
    motion = link_ref[:, 0:128]
    motion_before = link_ref[:, 128:256]
    outside = pltpu.roll(first_edge_ref[:, 128:256], 65, 1)
    motion_before = jnp.where((lane == 0) & initial, outside, motion_before)
    ends = (lane[0:1] == 63) & final & (shard == shards - 1)
    starts = (lane[0:1] == 0) & initial & (shard == 0)
    weight_after = jnp.where(ends, 0.0, motion[6:7])
    weight_before = jnp.where(starts, 0.0, motion_before[6:7])
    scratch[0:8] = weight_before * (current - previous - motion_before) - weight_after * (
        following - current - motion
    )
    scratch[8:16] = sums
    scratch[16:24] = half_turn(sums)
    f = [scratch[8 + 8 * (q % 2) + q // 2 : 9 + 8 * (q % 2) + q // 2, :] for q in range(16)]
    g = [f[k] + scratch[k : k + 1, :] for k in range(6)]
    diagonal = weight_after + weight_before + damping
    s, c, m = f[6] + diagonal, f[7:10], f[10:16]
    inverse = 1.0 / s
    d = [c[k] * inverse for k in range(3)]
    n00 = m[1] + m[2] + diagonal - (c[1] * d[1] + c[2] * d[2])
    n11 = m[0] + m[2] + diagonal - (c[0] * d[0] + c[2] * d[2])
    n22 = m[0] + m[1] + diagonal - (c[0] * d[0] + c[1] * d[1])
    n01, n02, n12 = c[0] * d[1] - m[3], c[0] * d[2] - m[4], c[1] * d[2] - m[5]
    b0 = g[0] - (d[1] * g[5] - d[2] * g[4])
    b1 = g[1] - (d[2] * g[3] - d[0] * g[5])
    b2 = g[2] - (d[0] * g[4] - d[1] * g[3])
    x0, x1, x2 = solve3(n00, n11, n22, n01, n02, n12, b0, b1, b2)
    x3 = (g[3] + (c[1] * x2 - c[2] * x1)) * inverse
    x4 = (g[4] + (c[2] * x0 - c[0] * x2)) * inverse
    x5 = (g[5] + (c[0] * x1 - c[1] * x0)) * inverse
    for k, x in enumerate((x0, x1, x2, x3, x4, x5)):
        scratch[k : k + 1, :] = x
    return current - scratch[0:8]


def new_points(sums_ref, near_ref):
    x = [near_ref[0, :, 0:128], half_turn(near_ref[0, :, 0:128]), near_ref[0, :, 128:256]]
    q = []
    for k in range(5):
        pair = total(sums_ref, k * 8)
        q += [pair, half_turn(pair)]
    moved = solve3(q[0] + damping, q[1] + damping, q[2] + damping, -q[3], -q[4], -q[5], q[6], q[7], q[8])
    return [x[k] - moved[k] for k in range(3)]


def total(sums_ref, row):
    parts = [sums_ref[d, row : row + 8, :] for d in range(sums_ref.shape[0])]
    while len(parts) > 1:
        parts = [p + q for p, q in zip(parts[0::2], parts[1::2])]
    return parts[0]


def load_all(sources, targets, sems):
    loads = [pltpu.make_async_copy(a, b, sems.at[n]) for n, (a, b) in enumerate(zip(sources, targets))]
    for load in loads:
        load.start()
    return loads


def wait_all(loads):
    for load in loads:
        load.wait()


def update_kernel(sums_ref, near_hbm, link_hbm, edge_hbm, copies_ref, sent_hbm, *scratch):
    near_ref, link_ref, edge_ref, sent, scratch, sems = scratch
    loads = load_all([near_hbm, link_hbm, edge_hbm], [near_ref, link_ref, edge_ref], sems)
    frames = total(sums_ref, 40)
    wait_all(loads)
    lower = lanes((8, 128)) < 64
    pose = new_poses(frames, near_ref, link_ref, edge_ref, edge_ref, scratch)
    sent[...] = pose
    send = pltpu.make_async_copy(sent, sent_hbm, sems.at[3])
    send.start()
    x = new_points(sums_ref, near_ref)
    left = jnp.where(lower, x[0], half_turn(x[1]))
    right = jnp.where(lower, x[2], half_turn(pose))
    for d in range(copies_ref.shape[0]):
        copies_ref[d, :, 0:128] = left
        copies_ref[d, :, 128:256] = right
    send.wait()


def last_poses_kernel(sums_ref, near_hbm, link_hbm, edge_hbm, first_edge_hbm, copies_ref, *scratch):
    near_ref, link_ref, edge_ref, first_edge_ref, scratch, sems = scratch
    sources = [near_hbm, link_hbm, edge_hbm, first_edge_hbm]
    loads = load_all(sources, [near_ref, link_ref, edge_ref, first_edge_ref], sems)
    frames = total(sums_ref, 40)
    wait_all(loads)
    pose = new_poses(frames, near_ref, link_ref, edge_ref, first_edge_ref, scratch)
    lower = lanes((1, 128)) < 64
    for h in range(3):
        pair = jnp.where(lower, pose[2 * h : 2 * h + 1], half_turn(pose[2 * h + 1 : 2 * h + 2]))
        for d in range(copies_ref.shape[0]):
            copies_ref[d, :, h * 128 : (h + 1) * 128] = pair


def last_points_kernel(sums_ref, near_hbm, out_ref, near_ref, sem):
    load = pltpu.make_async_copy(near_hbm, near_ref, sem)
    load.start()
    load.wait()
    x = new_points(sums_ref, near_ref)
    for k in range(3):
        for b in range(8):
            out_ref[k : k + 1, b * 64 : (b + 1) * 64] = x[k][b : b + 1, 0:64]


def spread_kernel(poses_ref, out_ref):
    for d in range(poses_ref.shape[0]):
        for k in range(6):
            out_ref[k : k + 1, d * 64 : (d + 1) * 64] = poses_ref[d, :, k * 64 : (k + 1) * 64]


def call(kernel, outs, scratch, args, spaces, room=48):
    space = {"s": pltpu.SMEM, "v": pltpu.VMEM, "h": pltpu.HBM}
    specs = [pl.BlockSpec(memory_space=space[letter]) for letter in spaces]
    return pl.pallas_call(
        kernel,
        out_shape=outs,
        in_specs=specs[: len(args)],
        out_specs=specs[len(args) :],
        scratch_shapes=scratch,
        compiler_params=pltpu.CompilerParams(vmem_limit_bytes=67_043_328 - (room << 20)),
    )(*args)


def exchange(array):
    return lax.all_to_all(array, "lm", 0, 0, tiled=True)


def on_device(
    camera_poses,
    landmarks,
    odometry,
    odometry_info,
    observations,
    tile_frame,
    tile_block,
    tile_count,
    block_slot,
):
    owners, shards = lax.axis_size("lm"), lax.axis_size("tm")
    slots = observations.shape[0]
    f32 = jnp.float32
    seen = jnp.transpose(observations, (1, 2, 3, 0))
    to_edges = []
    for a in range(shards - 1):
        to_edges.append((a * owners + owners - 1, (a + 1) * owners))
        to_edges.append(((a + 1) * owners, a * owners + owners - 1))

    def edges(array):
        return lax.ppermute(array, ("tm", "lm"), to_edges)

    def shape(*sizes):
        return jax.ShapeDtypeStruct(sizes, f32)

    def buffer(*sizes):
        return pltpu.VMEM(sizes, f32)

    dma = pltpu.SemaphoreType.DMA
    names = jax.ShapeDtypeStruct((8, 128), jnp.int32)
    copies, sent, link, *names = call(
        pack_kernel,
        [shape(owners, 8, 256), shape(8, 256), shape(8, 256), names, names],
        [
            buffer(*landmarks.shape),
            buffer(*camera_poses.shape),
            buffer(*odometry.shape),
            buffer(1, camera_poses.shape[1]),
            pltpu.VMEM((1, slots), jnp.int32),
            pltpu.VMEM((1, slots), jnp.int32),
            pltpu.VMEM(block_slot.shape, jnp.int32),
            buffer(8, 1024),
            buffer(8, 256),
            buffer(8, 256),
            buffer(8, 256),
            pltpu.VMEM((8, 128), jnp.int32),
            dma((11 + owners,)),
        ],
        [
            tile_count,
            landmarks,
            camera_poses,
            odometry,
            odometry_info[None, :],
            tile_frame[None, :],
            tile_block[None, :],
            block_slot,
        ],
        "shhhhhhhhhhhh",
        0,
    )
    (folded,) = call(
        fold_kernel,
        [jax.ShapeDtypeStruct((3, PLAIN, TILE, 128), seen.dtype)],
        [
            pltpu.VMEM(seen.shape, seen.dtype),
            pltpu.VMEM((3, PLAIN, TILE, 128), seen.dtype),
            dma((1 + 2 * GROUPS,)),
        ],
        [seen],
        "hh",
        12,
    )
    first_edge = None
    for iteration in range(ITERS):
        window = exchange(copies)
        edge = edges(sent)
        sums, near = call(
            tiles_kernel,
            [shape(owners, 48, 128), shape(3, 8, 256)],
            [
                buffer(3, 8, 256),
                pltpu.VMEM(folded.shape, folded.dtype),
                buffer(6 * PLAIN, 128),
                buffer(GROUPS * 192, 128),
                buffer(1024, 128),
                buffer(576, 128),
                buffer(owners, 48, 128),
                dma((8,)),
                dma((6,)),
            ],
            [window, names[iteration], folded],
            "vvhhh",
            12,
        )
        sums = exchange(sums)
        if iteration == 0:
            first_edge = edge
            copies, sent = call(
                update_kernel,
                [shape(owners, 8, 256), shape(8, 128)],
                [buffer(3, 8, 256), buffer(8, 256), buffer(8, 256), buffer(8, 128), buffer(24, 128), dma((4,))],
                [sums, near, link, edge],
                "vhhhvh",
            )
    (copies,) = call(
        last_poses_kernel,
        [shape(owners, 1, 384)],
        [buffer(3, 8, 256), buffer(8, 256), buffer(8, 128), buffer(8, 256), buffer(24, 128), dma((4,))],
        [sums, near, link, edge, first_edge],
        "vhhhhv",
    )
    gathered = exchange(copies)
    (points,) = call(
        last_points_kernel, [shape(*landmarks.shape)], [buffer(3, 8, 256), dma], [sums, near], "vhv"
    )
    (poses,) = call(spread_kernel, [shape(*camera_poses.shape)], [], [gathered], "vv")
    return (poses, points)


def solution(mesh):
    return jax.shard_map(
        on_device,
        mesh=mesh,
        in_specs=(
            P(None, "tm"),
            P(None, ("tm", "lm")),
            P(None, "tm"),
            P("tm"),
            P(("tm", "lm"), None, None, None),
            P(("tm", "lm")),
            P(("tm", "lm")),
            P(("tm", "lm")),
            P("tm", None),
        ),
        out_specs=(P(None, "tm"), P(None, ("tm", "lm"))),
        check_vma=False,
    )
```

time: 112 us -> 102 us (0.911)
  local copies, waits for them, and re-layouts: 12.4 us -> 0.02 us
  Pallas kernels: 22.1 us -> 29.2 us
  waiting for transfers between devices: 41.8 us -> 36.4 us
    unnamed x38 -> x8, local copies, waits for them, and re-layouts: 12.4 us -> 0.02 us
    pallas_call x7 -> x8, Pallas kernels: 22.1 us -> 29.2 us  [call(): pl.pallas_call(kernel, out_shape=outs, in_specs=specs[:len(args)], out_sp...]
    all_to_all x4, waiting for transfers between devices: 41.8 us -> 36.4 us  [exchange(): return lax.all_to_all(array, 'lm', 0, 0, tiled=True)]
  transfers between devices with their start and end apart: 6 -> 6, of which waited for: 4 -> 4; matrix products, arithmetic and copies ran while one was open for 0% -> 0% of each run, Pallas kernels for 1% -> 7%
where the time goes in v2:
time: 102 us; the launch traced here: 101 us
  waiting for transfers between devices  36.4 us (36%)
  Pallas kernels  29.2 us (29%)
  starting transfers between devices  22.7 us (22%)
  blocking collectives  11.6 us (11%)
  between operations  1.42 us (1%)
    all_to_all x4, waiting for transfers between devices, exchange(): return lax.all_to_all(array, 'lm', 0, 0, tiled=True)  36.4 us
    pallas_call x8, Pallas kernels, call(): pl.pallas_call(kernel, out_shape=outs, in_specs=specs[:len(args)], out_sp...  29.2 us
    all_to_all x4, starting transfers between devices, exchange(): return lax.all_to_all(array, 'lm', 0, 0, tiled=True)  21.4 us
    all_to_all x1, blocking collectives, exchange(): return lax.all_to_all(array, 'lm', 0, 0, tiled=True)  11.6 us
  transfers between devices with their start and end apart: 6, of which 4 were waited for; matrix products, arithmetic and copies ran while one was open for 0% of the time, Pallas kernels for 7%

profile of v2, /device:TPU:1, one launch (start us, length us, event | category | flops | bytes accessed | tf_op | source)
XLA Modules:
  0.0 101.3 jit_solution(13617924239934423914)
XLA Ops:
  1.3 1.9 %shard_map.104 = (f32[16,8,256]{2,1,0:T(8,128)}, f32[8,256]{1,0:T(8,128)}, f32[8,256]{1,0:T(8,128)}, s32[8,128]{1,0:T(8,128)}, s32[8,128]{1,0:T(8,128)}) custom-call(s32[1]{0:T(128)S(6)} %copy.11.count_ref, f32[3,512]{1,0:T(4,128)} %points_hbm.1, f32[6,1024]{1,0:T(8,128)} %poses_hbm.1, f32[6,1024]{1,0:T(8,128)} %odometry_hbm.1, f32[1,1024]{1,0:T(1,128)} %bitcast.5, ...), custom_call_target="tpu_custom_call" | custom-call | tf_op jit(solution)/shard_map/pallas_call | solution.py:458
  3.2 0.0 copy-start.2
  3.2 10.1 %all-to-all-start = ((f32[16,8,256]{2,1,0:T(8,128)}), f32[16,8,256]{2,1,0:T(8,128)S(1)}, u32[]{:S(2)}, u32[]{:S(2)}) async-start(f32[16,8,256]{2,1,0:T(8,128)} %get-tuple-element.13), calls=%async_computation | async-start | bytes 262144 | tf_op jit(solution)/shard_map/all_to_all | solution.py:469
  13.4 0.0 copy-start.3
  13.4 0.0 copy-start
  13.4 6.2 %shard_map.105.seen_hbm = bf16[3,48,64,128]{3,2,1,0:T(8,128)(2,1)} custom-call(bf16[3,64,64,96]{3,2,1,0:T(8,128)(2,1)} %bitcast.4), custom_call_target="tpu_custom_call" | custom-call | tf_op jit(solution)/shard_map/pallas_call | solution.py:458
  19.6 0.0 copy-start.1
  19.6 2.9 %all-to-all-done.window_ref = f32[16,8,256]{2,1,0:T(8,128)S(1)} async-done(((f32[16,8,256]{2,1,0:T(8,128)}), f32[16,8,256]{2,1,0:T(8,128)S(1)}, u32[]{:S(2)}, u32[]{:S(2)}) %all-to-all-start) | async-done | bytes 131104 | tf_op jit(solution)/shard_map/all_to_all | solution.py:469
  22.6 0.0 copy-done.2
  22.6 9.1 %shard_map.106 = (f32[16,48,128]{2,1,0:T(8,128)}, f32[3,8,256]{2,1,0:T(8,128)S(1)}) custom-call(f32[16,8,256]{2,1,0:T(8,128)S(1)} %all-to-all-done.window_ref, s32[8,128]{1,0:T(8,128)S(1)} %copy-done.2, bf16[3,48,64,128]{3,2,1,0:T(8,128)(2,1)} %shard_map.105.seen_hbm), custom_call_target="tpu_custom_call" | custom-call | tf_op jit(solution)/shard_map/pallas_call | solution.py:458
  31.6 4.4 %all-to-all-start.1 = ((f32[16,48,128]{2,1,0:T(8,128)}), f32[16,48,128]{2,1,0:T(8,128)S(1)}, u32[]{:S(2)}, u32[]{:S(2)}) async-start(f32[16,48,128]{2,1,0:T(8,128)} %get-tuple-element.15), calls=%async_computation.1 | async-start | bytes 786432 | tf_op jit(solution)/shard_map/all_to_all | solution.py:469
  36.0 0.0 copy-done.3
  36.0 0.7 collective-permute-start
  36.7 0.0 collective-permute-done.edge_hbm.first_edge_hbm
  36.7 13.8 %all-to-all-done.1.sums_ref = f32[16,48,128]{2,1,0:T(8,128)S(1)} async-done(((f32[16,48,128]{2,1,0:T(8,128)}), f32[16,48,128]{2,1,0:T(8,128)S(1)}, u32[]{:S(2)}, u32[]{:S(2)}) %all-to-all-start.1) | async-done | bytes 393248 | tf_op jit(solution)/shard_map/all_to_all | solution.py:469
  50.5 0.0 copy-done
  50.5 0.4 shard_map.107
  51.0 11.6 %all_to_all.25.window_ref = f32[16,8,256]{2,1,0:T(8,128)S(1)} all-to-all(f32[16,8,256]{2,1,0:T(8,128)S(1)} %get-tuple-element.19), channel_id=1, replica_groups=mesh['tm'=32,'lm'=16] {'lm'}, dimensions={0} | all-to-all | bytes 262144 | tf_op jit(solution)/shard_map/all_to_all | solution.py:469
  62.5 0.0 copy-done.1
  62.5 9.1 %shard_map.108 = (f32[16,48,128]{2,1,0:T(8,128)}, f32[3,8,256]{2,1,0:T(8,128)S(1)}) custom-call(f32[16,8,256]{2,1,0:T(8,128)S(1)} %all_to_all.25.window_ref, s32[8,128]{1,0:T(8,128)S(1)} %copy-done.1, bf16[3,48,64,128]{3,2,1,0:T(8,128)(2,1)} %shard_map.105.seen_hbm), custom_call_target="tpu_custom_call" | custom-call | tf_op jit(solution)/shard_map/pallas_call | solution.py:458
  71.6 3.5 %all-to-all-start.3 = ((f32[16,48,128]{2,1,0:T(8,128)}), f32[16,48,128]{2,1,0:T(8,128)S(1)}, u32[]{:S(2)}, u32[]{:S(2)}) async-start(f32[16,48,128]{2,1,0:T(8,128)} %get-tuple-element.21), calls=%async_computation.3 | async-start | bytes 786432 | tf_op jit(solution)/shard_map/all_to_all | solution.py:469
  75.1 0.7 collective-permute-start.1
  75.7 0.0 collective-permute-done.1.edge_hbm
  75.7 13.7 %all-to-all-done.3.sums_ref = f32[16,48,128]{2,1,0:T(8,128)S(1)} async-done(((f32[16,48,128]{2,1,0:T(8,128)}), f32[16,48,128]{2,1,0:T(8,128)S(1)}, u32[]{:S(2)}, u32[]{:S(2)}) %all-to-all-start.3) | async-done | bytes 393248 | tf_op jit(solution)/shard_map/all_to_all | solution.py:469
  89.4 0.9 shard_map.109
  90.4 3.4 %all-to-all-start.4 = ((f32[16,1,384]{2,1,0:T(1,128)}), f32[16,1,384]{2,1,0:T(1,128)S(1)}, u32[]{:S(2)}, u32[]{:S(2)}) async-start(f32[16,1,384]{2,1,0:T(1,128)} %shard_map.109), calls=%async_computation.4 | async-start | bytes 49152 | tf_op jit(solution)/shard_map/all_to_all | solution.py:469
  93.8 0.8 shard_map.111
  94.6 5.9 %all-to-all-done.4.poses_ref = f32[16,1,384]{2,1,0:T(1,128)S(1)} async-done(((f32[16,1,384]{2,1,0:T(1,128)}), f32[16,1,384]{2,1,0:T(1,128)S(1)}, u32[]{:S(2)}, u32[]{:S(2)}) %all-to-all-start.4) | async-done | bytes 24608 | tf_op jit(solution)/shard_map/all_to_all | solution.py:469
  100.6 0.7 shard_map.110
Async XLA Ops:
  3.2 19.3 %copy-start.2 = (s32[8,128]{1,0:T(8,128)S(1)}, s32[8,128]{1,0:T(8,128)}, u32[]{:S(2)}) copy-start(s32[8,128]{1,0:T(8,128)} %get-tuple-element.14.names_ref) | copy-start | bytes 12292
  3.2 19.3 %all-to-all-start = ((f32[16,8,256]{2,1,0:T(8,128)}), f32[16,8,256]{2,1,0:T(8,128)S(1)}, u32[]{:S(2)}, u32[]{:S(2)}) async-start(f32[16,8,256]{2,1,0:T(8,128)} %get-tuple-element.13), calls=%async_computation | async-start | bytes 262144 | tf_op jit(solution)/shard_map/all_to_all | solution.py:469
  13.4 22.6 %copy-start.3 = (f32[8,256]{1,0:T(8,128)S(1)}, f32[8,256]{1,0:T(8,128)}, u32[]{:S(2)}) copy-start(f32[8,256]{1,0:T(8,128)} %get-tuple-element.18) | copy-start | bytes 24580
  13.4 37.1 %copy-start = (f32[8,256]{1,0:T(8,128)S(1)}, f32[8,256]{1,0:T(8,128)}, u32[]{:S(2)}) copy-start(f32[8,256]{1,0:T(8,128)} %get-tuple-element.17.link_hbm) | copy-start | bytes 24580
  19.6 42.9 %copy-start.1 = (s32[8,128]{1,0:T(8,128)S(1)}, s32[8,128]{1,0:T(8,128)}, u32[]{:S(2)}) copy-start(s32[8,128]{1,0:T(8,128)} %get-tuple-element.20.names_ref) | copy-start | bytes 12292
  31.6 18.9 %all-to-all-start.1 = ((f32[16,48,128]{2,1,0:T(8,128)}), f32[16,48,128]{2,1,0:T(8,128)S(1)}, u32[]{:S(2)}, u32[]{:S(2)}) async-start(f32[16,48,128]{2,1,0:T(8,128)} %get-tuple-element.15), calls=%async_computation.1 | async-start | bytes 786432 | tf_op jit(solution)/shard_map/all_to_all | solution.py:469
  36.0 0.7 collective-permute-start
  71.6 17.8 %all-to-all-start.3 = ((f32[16,48,128]{2,1,0:T(8,128)}), f32[16,48,128]{2,1,0:T(8,128)S(1)}, u32[]{:S(2)}, u32[]{:S(2)}) async-start(f32[16,48,128]{2,1,0:T(8,128)} %get-tuple-element.21), calls=%async_computation.3 | async-start | bytes 786432 | tf_op jit(solution)/shard_map/all_to_all | solution.py:469
  75.1 0.7 collective-permute-start.1
  90.4 10.2 %all-to-all-start.4 = ((f32[16,1,384]{2,1,0:T(1,128)}), f32[16,1,384]{2,1,0:T(1,128)S(1)}, u32[]{:S(2)}, u32[]{:S(2)}) async-start(f32[16,1,384]{2,1,0:T(1,128)} %shard_map.109), calls=%async_computation.4 | async-start | bytes 49152 | tf_op jit(solution)/shard_map/all_to_all | solution.py:469

commit v3 on v2

--- a/solution.py
+++ b/solution.py
@@ -14,6 +14,7 @@
 GROUPS = SLOTS // EXTRA
 PLAIN = TILE * SLOTS // 128
 FOLDED = TILE - PLAIN
+PARTS = 2
 damping = 1.0
 scale = 4.0
 
@@ -31,6 +32,18 @@
     for h in range(8):
         pair = jnp.where(block // 2 == h, ref[:, h * 128 : (h + 1) * 128], pair)
     return jnp.where(block % 2 == 1, half_turn(pair), pair)
+
+
+def load_all(sources, targets, sems):
+    loads = [pltpu.make_async_copy(a, b, sems.at[n]) for n, (a, b) in enumerate(zip(sources, targets))]
+    for load in loads:
+        load.start()
+    return loads
+
+
+def wait_all(loads):
+    for load in loads:
+        load.wait()
 
 
 def pack_kernel(
@@ -143,7 +156,7 @@
     return lax.dot_general(a, b, (((1,), (1,)), ((), ())), preferred_element_type=jnp.float32)
 
 
-def fold_kernel(seen_hbm, out_hbm, seen, folded, sems):
+def fold_kernel(seen_hbm, folded, seen, sems):
     parts = [pl.ds(PLAIN, FOLDED)] + [pl.ds(g * FOLDED, FOLDED) for g in range(GROUPS)]
     loads = [
         pltpu.make_async_copy(seen_hbm.at[:, part], seen.at[:, part], sems.at[n]) for n, part in enumerate(parts)
@@ -151,7 +164,6 @@
     for load in loads:
         load.start()
     loads[0].wait()
-    stores = []
     for g in range(GROUPS):
         loads[1 + g].wait()
 
@@ -164,30 +176,24 @@
             return carry
 
         lax.fori_loop(0, FOLDED, step, 0)
-        part = parts[1 + g]
-        stores.append(pltpu.make_async_copy(folded.at[:, part], out_hbm.at[:, part], sems.at[1 + GROUPS + g]))
-        stores[-1].start()
-    for store in stores:
-        store.wait()
-
-
-def tiles_kernel(window_ref, names_ref, seen_hbm, out_hbm, near_hbm, *scratch):
-    near_ref, seen_ref, pose, point, fsum, psum, sums, sems, load_sems = scratch
+
+
+def unfold(parts):
+    lane = lanes(parts.shape[1:])
+    result = jnp.where(lane < SLOTS, sum(parts[g] for g in range(GROUPS)), 0.0)
+    for g in range(GROUPS):
+        mine = (lane >= g * EXTRA) & (lane < (g + 1) * EXTRA)
+        result = result + jnp.where(mine, pltpu.roll(parts[g], (g + 1) * EXTRA, 1), 0.0)
+    return result
+
+
+def tiles_kernel(window_ref, names_ref, seen_ref, out_hbm, near_hbm, *scratch):
+    near_ref, pose, point, fsum, psum, partial, right, sums, sems = scratch
     owner, owners = lax.axis_index("lm"), lax.axis_size("lm")
-    chunks = load_sems.shape[0]
-    pieces = PLAIN // chunks
-
-    def load(n):
-        part = pl.ds(n * pieces, pieces)
-        return pltpu.make_async_copy(seen_hbm.at[:, part], seen_ref.at[:, part], load_sems.at[n])
-
-    ahead = 2
-    for n in range(ahead):
-        load(n).start()
     near_ref[0] = window_ref[owner]
     near_ref[1] = window_ref[jnp.maximum(owner - 1, 0)]
     near_ref[2] = window_ref[jnp.minimum(owner + 1, owners - 1)]
-    turned = split(jnp.transpose(window_ref[...].reshape(128, 256), (1, 0)), 3)
+    turned = split(jnp.transpose(window_ref[...].reshape(128, 256), (1, 0)), PARTS)
     put_near = pltpu.make_async_copy(near_ref, near_hbm, sems.at[7])
     put_near.start()
     row = lax.broadcasted_iota(jnp.int32, (128, 128), 0)
@@ -197,19 +203,38 @@
         frame, position = names_ref[2 + g : 3 + g, :], names_ref[2 + GROUPS + g : 3 + GROUPS + g, :]
         pick = jnp.where(position == row, 1.0, 0.0).astype(jnp.bfloat16)
         found = dot(points, pick)
-        point[g * 192 : (g + 1) * 192, :] = found[0:192] + (found[192:384] + found[384:576])
+        point[g * 192 : (g + 1) * 192, :] = sum(found[n * 192 : (n + 1) * 192] for n in range(PARTS))
         at = 192 + g * FOLDED
         poses = jnp.concatenate(
             [piece[r : r + FOLDED] for r in (at, 192 + PLAIN) for piece in turned], axis=0
         )
         for k in range(6):
             pick = jnp.where(frame * 8 + k == row, 1.0, 0.0).astype(jnp.bfloat16)
-            found = [dot(poses, pick)[n * FOLDED : (n + 1) * FOLDED] for n in range(6)]
-            found = [found[n] + (found[n + 1] + found[n + 2]) for n in (0, 3)]
+            both = dot(poses, pick)
+            found = [both[n * FOLDED : (n + 1) * FOLDED] for n in range(2 * PARTS)]
+            found = [sum(found[:PARTS]), sum(found[PARTS:])]
             pose[k * PLAIN + g * FOLDED : k * PLAIN + (g + 1) * FOLDED, :] = jnp.where(lane < SLOTS, *found)
     psum[...] = jnp.zeros_like(psum)
+    partial[...] = jnp.zeros_like(partial)
+
+    sub = lax.broadcasted_iota(jnp.int32, (8, 128), 0)
+
+    def merge(a, b, shift):
+        low = (sub // shift) % 2 == 0
+        if shift == 4:
+            return jnp.where(low, a, b) + pltpu.roll(jnp.where(low, b, a), 4, 0)
+        return jnp.where(low, a + pltpu.roll(a, 8 - shift, 0), b + pltpu.roll(b, shift, 0))
+
+    def finish(i):
+        for half in range(2):
+            parts = [partial[(half * 8 + q) * 8 : (half * 8 + q + 1) * 8, :] for q in range(8)]
+            for shift in (4, 2, 1):
+                count = len(parts) // 2
+                parts = [merge(parts[q], parts[q + count], shift) for q in range(count)]
+            fsum[pl.ds(pl.multiple_of(i * 16 + half * 8, 8), 8), :] = parts[0]
 
     def step(g, i, carry):
+        finish(jnp.maximum(i - 1, 0))
         w = [jnp.broadcast_to(pose[pl.ds(k * PLAIN + i, 1), :], (8, 128)) for k in range(3)]
         t = [jnp.broadcast_to(pose[pl.ds((3 + k) * PLAIN + i, 1), :], (8, 128)) for k in range(3)]
         w00, w11, w22 = w[0] * w[0], w[1] * w[1], w[2] * w[2]
@@ -259,57 +284,50 @@
                     c2 - (w[0] * c1 - w[1] * c0),
                 ]
                 for q, term in enumerate(terms):
-                    psum[q * 64 + at : q * 64 + at + 8, :] += term
+                    psum[g, q * 64 + at : q * 64 + at + 8, :] += term
         for q in range(16):
-            fsum[pl.ds(q * 64 + i, 1), :] = jnp.sum(total[q], axis=0, keepdims=True)
+            partial[q * 8 : (q + 1) * 8, :] = total[q]
         return carry
 
-    def chunk(g, n, carry):
-        load(n).wait()
-
-        @pl.when(n + ahead < chunks)
-        def _():
-            load(n + ahead).start()
-
-        return lax.fori_loop(n * pieces, (n + 1) * pieces, functools.partial(step, g), carry)
-
-    lane = lanes((64, 128))
-    each = chunks // GROUPS
     for g in range(GROUPS):
-        lax.fori_loop(g * each, (g + 1) * each, functools.partial(chunk, g), 0)
-        mine = (lane >= g * EXTRA) & (lane < (g + 1) * EXTRA)
-        for q in range(9):
-            part = psum[q * 64 : (q + 1) * 64, :]
-            back = jnp.where(mine, pltpu.roll(part, (g + 1) * EXTRA, 1), 0.0)
-            psum[q * 64 : (q + 1) * 64, :] = jnp.where(lane < SLOTS, part, 0.0) + back
-    lane = lanes((FOLDED, 128))
+        lax.fori_loop(g * FOLDED, (g + 1) * FOLDED, functools.partial(step, g), 0)
+    finish(PLAIN - 1)
+    frame_sums = []
     for q in range(16):
+        rows = fsum[pl.ds(q, PLAIN, stride=16), :]
         back = jnp.zeros((FOLDED, 128), jnp.float32)
         for g in range(GROUPS):
-            part = fsum[q * 64 + g * FOLDED : q * 64 + (g + 1) * FOLDED, :]
-            back = jnp.where((lane >= g * EXTRA) & (lane < (g + 1) * EXTRA), pltpu.roll(part, (g + 1) * EXTRA, 1), back)
-        fsum[q * 64 + PLAIN : (q + 1) * 64, :] = back
+            mine = (lane >= g * EXTRA) & (lane < (g + 1) * EXTRA)
+            back = jnp.where(mine, pltpu.roll(rows[g * FOLDED : (g + 1) * FOLDED], (g + 1) * EXTRA, 1), back)
+        frame_sums += [rows, back]
     frame, position = names_ref[0:1, :], names_ref[1:2, :]
     held = position == row
     own = jnp.where(frame == lax.broadcasted_iota(jnp.int32, (16, 128), 0), scale, 0.0).astype(jnp.bfloat16)
-    frames = sum(dot_t(own, piece) for piece in split(fsum[...], 3))
-    for r in range(8):
-        sums[:, 40 + r, :] = frames[:, r * 128 : (r + 1) * 128]
+    frames = sum(dot_t(own, piece) for piece in split(jnp.concatenate(frame_sums, axis=0), PARTS))
+    for r in range(4):
+        pair = frames[:, r * 128 : (r + 1) * 128]
+        right[:, 2 * r, :] = half_turn(pair)
+        right[:, 2 * r + 1, :] = pair
+        sums[:, 10, r, :] = frames[:, (4 + r) * 128 : (5 + r) * 128]
     put_near.wait()
-    stores = [pltpu.make_async_copy(sums.at[:, 40:48], out_hbm.at[:, 40:48], sems.at[5])]
+    stores = [pltpu.make_async_copy(sums.at[:, 10], out_hbm.at[:, 10], sems.at[5])]
     stores[0].start()
     own = jnp.where(held, scale, 0.0).astype(jnp.bfloat16)
     for q in range(5):
         wide = 128 if q < 4 else 64
-        part = sum(dot_t(own, piece) for piece in split(psum[q * 128 : q * 128 + wide, :], 3))
+        part = unfold(psum[:, q * 128 : q * 128 + wide, :])
+        part = sum(dot_t(own, piece) for piece in split(part, PARTS))
         if wide < 128:
             part = jnp.concatenate([part, jnp.zeros_like(part)], axis=1)
-        rows = slice(q * 8, (q + 1) * 8)
-        sums[:, rows, :] = part.reshape(16, 8, 128)
+        part = part.reshape(16, 8, 128)
+        if wide < 128:
+            part = jnp.where(lax.broadcasted_iota(jnp.int32, part.shape, 2) < 64, part, right[...])
+        sums[:, 2 * q] = part[:, 0:4]
+        sums[:, 2 * q + 1] = part[:, 4:8]
+        rows = slice(2 * q, 2 * q + 2)
         stores.append(pltpu.make_async_copy(sums.at[:, rows], out_hbm.at[:, rows], sems.at[q]))
         stores[-1].start()
-    for store in stores:
-        store.wait()
+    wait_all(stores)
 
 
 def solve3(m00, m11, m22, m01, m02, m12, b0, b1, b2):
@@ -328,7 +346,7 @@
     return x0, x1, x2
 
 
-def new_poses(sums, near_ref, link_ref, edge_ref, first_edge_ref, scratch):
+def new_poses(lower_sums, upper_sums, near_ref, link_ref, edge_ref, first_edge_ref, scratch):
     owner, shard = lax.axis_index("lm"), lax.axis_index("tm")
     owners, shards = lax.axis_size("lm"), lax.axis_size("tm")
     lane = lanes((8, 128))
@@ -350,9 +368,12 @@
     scratch[0:8] = weight_before * (current - previous - motion_before) - weight_after * (
         following - current - motion
     )
-    scratch[8:16] = sums
-    scratch[16:24] = half_turn(sums)
-    f = [scratch[8 + 8 * (q % 2) + q // 2 : 9 + 8 * (q % 2) + q // 2, :] for q in range(16)]
+    scratch[8:16] = half_turn(lower_sums)
+    scratch[16:20] = upper_sums
+    scratch[20:24] = half_turn(upper_sums)
+    f = [scratch[8 + q : 9 + q, :] for q in range(8)]
+    for r in range(4):
+        f += [scratch[16 + r : 17 + r, :], scratch[20 + r : 21 + r, :]]
     g = [f[k] + scratch[k : k + 1, :] for k in range(6)]
     diagonal = weight_after + weight_before + damping
     s, c, m = f[6] + diagonal, f[7:10], f[10:16]
@@ -374,46 +395,37 @@
     return current - scratch[0:8]
 
 
-def new_points(sums_ref, near_ref):
+def new_points(sums, near_ref):
     x = [near_ref[0, :, 0:128], half_turn(near_ref[0, :, 0:128]), near_ref[0, :, 128:256]]
     q = []
-    for k in range(5):
-        pair = total(sums_ref, k * 8)
+    for pair in sums:
         q += [pair, half_turn(pair)]
     moved = solve3(q[0] + damping, q[1] + damping, q[2] + damping, -q[3], -q[4], -q[5], q[6], q[7], q[8])
     return [x[k] - moved[k] for k in range(3)]
 
 
-def total(sums_ref, row):
-    parts = [sums_ref[d, row : row + 8, :] for d in range(sums_ref.shape[0])]
+def total(sums_ref, part):
+    parts = [sums_ref[d, part] for d in range(sums_ref.shape[0])]
     while len(parts) > 1:
         parts = [p + q for p, q in zip(parts[0::2], parts[1::2])]
     return parts[0]
 
 
-def load_all(sources, targets, sems):
-    loads = [pltpu.make_async_copy(a, b, sems.at[n]) for n, (a, b) in enumerate(zip(sources, targets))]
-    for load in loads:
-        load.start()
-    return loads
-
-
-def wait_all(loads):
-    for load in loads:
-        load.wait()
+def pair_total(sums_ref, k):
+    return jnp.concatenate([total(sums_ref, 2 * k), total(sums_ref, 2 * k + 1)], axis=0)
 
 
 def update_kernel(sums_ref, near_hbm, link_hbm, edge_hbm, copies_ref, sent_hbm, *scratch):
     near_ref, link_ref, edge_ref, sent, scratch, sems = scratch
     loads = load_all([near_hbm, link_hbm, edge_hbm], [near_ref, link_ref, edge_ref], sems)
-    frames = total(sums_ref, 40)
+    frames = pair_total(sums_ref, 4), total(sums_ref, 10)
     wait_all(loads)
     lower = lanes((8, 128)) < 64
-    pose = new_poses(frames, near_ref, link_ref, edge_ref, edge_ref, scratch)
+    pose = new_poses(*frames, near_ref, link_ref, edge_ref, edge_ref, scratch)
     sent[...] = pose
     send = pltpu.make_async_copy(sent, sent_hbm, sems.at[3])
     send.start()
-    x = new_points(sums_ref, near_ref)
+    x = new_points([pair_total(sums_ref, k) for k in range(4)] + [frames[0]], near_ref)
     left = jnp.where(lower, x[0], half_turn(x[1]))
     right = jnp.where(lower, x[2], half_turn(pose))
     for d in range(copies_ref.shape[0]):
@@ -426,9 +438,9 @@
     near_ref, link_ref, edge_ref, first_edge_ref, scratch, sems = scratch
     sources = [near_hbm, link_hbm, edge_hbm, first_edge_hbm]
     loads = load_all(sources, [near_ref, link_ref, edge_ref, first_edge_ref], sems)
-    frames = total(sums_ref, 40)
+    frames = pair_total(sums_ref, 4), total(sums_ref, 10)
     wait_all(loads)
-    pose = new_poses(frames, near_ref, link_ref, edge_ref, first_edge_ref, scratch)
+    pose = new_poses(*frames, near_ref, link_ref, edge_ref, first_edge_ref, scratch)
     lower = lanes((1, 128)) < 64
     for h in range(3):
         pair = jnp.where(lower, pose[2 * h : 2 * h + 1], half_turn(pose[2 * h + 1 : 2 * h + 2]))
@@ -439,8 +451,9 @@
 def last_points_kernel(sums_ref, near_hbm, out_ref, near_ref, sem):
     load = pltpu.make_async_copy(near_hbm, near_ref, sem)
     load.start()
+    sums = [pair_total(sums_ref, k) for k in range(5)]
     load.wait()
-    x = new_points(sums_ref, near_ref)
+    x = new_points(sums, near_ref)
     for k in range(3):
         for b in range(8):
             out_ref[k : k + 1, b * 64 : (b + 1) * 64] = x[k][b : b + 1, 0:64]
@@ -536,12 +549,11 @@
         [jax.ShapeDtypeStruct((3, PLAIN, TILE, 128), seen.dtype)],
         [
             pltpu.VMEM(seen.shape, seen.dtype),
-            pltpu.VMEM((3, PLAIN, TILE, 128), seen.dtype),
-            dma((1 + 2 * GROUPS,)),
+            dma((1 + GROUPS,)),
         ],
         [seen],
-        "hh",
-        12,
+        "hv",
+        14,
     )
     first_edge = None
     for iteration in range(ITERS):
@@ -549,21 +561,21 @@
         edge = edges(sent)
         sums, near = call(
             tiles_kernel,
-            [shape(owners, 48, 128), shape(3, 8, 256)],
+            [shape(owners, 11, 4, 128), shape(3, 8, 256)],
             [
                 buffer(3, 8, 256),
-                pltpu.VMEM(folded.shape, folded.dtype),
                 buffer(6 * PLAIN, 128),
                 buffer(GROUPS * 192, 128),
-                buffer(1024, 128),
-                buffer(576, 128),
-                buffer(owners, 48, 128),
+                buffer(16 * PLAIN, 128),
+                buffer(GROUPS, 576, 128),
+                buffer(128, 128),
+                buffer(owners, 8, 128),
+                buffer(owners, 11, 4, 128),
                 dma((8,)),
-                dma((6,)),
             ],
             [window, names[iteration], folded],
-            "vvhhh",
-            12,
+            "vvvhh",
+            14,
         )
         sums = exchange(sums)
         if iteration == 0:

time: 102 us -> 97 us (0.951)
  Pallas kernels: 29.2 us -> 25.8 us
    pallas_call x8, Pallas kernels: 29.2 us -> 25.8 us  [call(): pl.pallas_call(kernel, out_shape=outs, in_specs=specs[:len(args)], out_sp...]
  transfers between devices with their start and end apart: 6 -> 6, of which waited for: 4 -> 4; matrix products, arithmetic and copies ran while one was open for 0% -> 0% of each run, Pallas kernels for 7% -> 6%
where the time goes in v3:
time: 97 us; the launch traced here: 96.4 us
  waiting for transfers between devices  35.8 us (37%)
  Pallas kernels  25.8 us (27%)
  starting transfers between devices  21.8 us (22%)
  blocking collectives  11.6 us (12%)
  between operations  1.42 us (1%)
    all_to_all x4, waiting for transfers between devices, exchange(): return lax.all_to_all(array, 'lm', 0, 0, tiled=True)  35.8 us
    pallas_call x8, Pallas kernels, call(): pl.pallas_call(kernel, out_shape=outs, in_specs=specs[:len(args)], out_sp...  25.8 us
    all_to_all x4, starting transfers between devices, exchange(): return lax.all_to_all(array, 'lm', 0, 0, tiled=True)  20.5 us
    all_to_all x1, blocking collectives, exchange(): return lax.all_to_all(array, 'lm', 0, 0, tiled=True)  11.6 us
  transfers between devices with their start and end apart: 6, of which 4 were waited for; matrix products, arithmetic and copies ran while one was open for 0% of the time, Pallas kernels for 6%

profile of v3, /device:TPU:1, one launch (start us, length us, event | category | flops | bytes accessed | tf_op | source)
XLA Modules:
  0.0 96.4 jit_solution(16253228903742658472)
XLA Ops:
  1.3 1.9 %shard_map.104 = (f32[16,8,256]{2,1,0:T(8,128)}, f32[8,256]{1,0:T(8,128)}, f32[8,256]{1,0:T(8,128)}, s32[8,128]{1,0:T(8,128)}, s32[8,128]{1,0:T(8,128)}) custom-call(s32[1]{0:T(128)S(6)} %copy.11.count_ref, f32[3,512]{1,0:T(4,128)} %points_hbm.1, f32[6,1024]{1,0:T(8,128)} %poses_hbm.1, f32[6,1024]{1,0:T(8,128)} %odometry_hbm.1, f32[1,1024]{1,0:T(1,128)} %bitcast.5, ...), custom_call_target="tpu_custom_call" | custom-call | tf_op jit(solution)/shard_map/pallas_call | solution.py:471
  3.2 0.0 copy-start.2
  3.2 10.1 %all-to-all-start = ((f32[16,8,256]{2,1,0:T(8,128)}), f32[16,8,256]{2,1,0:T(8,128)S(1)}, u32[]{:S(2)}, u32[]{:S(2)}) async-start(f32[16,8,256]{2,1,0:T(8,128)} %get-tuple-element.13), calls=%async_computation | async-start | bytes 262144 | tf_op jit(solution)/shard_map/all_to_all | solution.py:482
  13.4 0.0 copy-start.3
  13.4 0.0 copy-start
  13.4 5.3 %shard_map.105.seen_ref = bf16[3,48,64,128]{3,2,1,0:T(8,128)(2,1)S(1)} custom-call(bf16[3,64,64,96]{3,2,1,0:T(8,128)(2,1)} %bitcast.4), custom_call_target="tpu_custom_call" | custom-call | tf_op jit(solution)/shard_map/pallas_call | solution.py:471
  18.7 0.0 copy-start.1
  18.7 3.8 %all-to-all-done.window_ref = f32[16,8,256]{2,1,0:T(8,128)S(1)} async-done(((f32[16,8,256]{2,1,0:T(8,128)}), f32[16,8,256]{2,1,0:T(8,128)S(1)}, u32[]{:S(2)}, u32[]{:S(2)}) %all-to-all-start) | async-done | bytes 131104 | tf_op jit(solution)/shard_map/all_to_all | solution.py:482
  22.6 0.0 copy-done.2
  22.6 7.8 %shard_map.106 = (f32[16,11,4,128]{3,2,1,0:T(4,128)}, f32[3,8,256]{2,1,0:T(8,128)S(1)}) custom-call(f32[16,8,256]{2,1,0:T(8,128)S(1)} %all-to-all-done.window_ref, s32[8,128]{1,0:T(8,128)S(1)} %copy-done.2, bf16[3,48,64,128]{3,2,1,0:T(8,128)(2,1)S(1)} %shard_map.105.seen_ref), custom_call_target="tpu_custom_call" | custom-call | tf_op jit(solution)/shard_map/pallas_call | solution.py:471
  30.3 3.5 %all-to-all-start.1 = ((f32[16,11,4,128]{3,2,1,0:T(4,128)}), f32[16,11,4,128]{3,2,1,0:T(4,128)S(1)}, u32[]{:S(2)}, u32[]{:S(2)}) async-start(f32[16,11,4,128]{3,2,1,0:T(4,128)} %get-tuple-element.15), calls=%async_computation.1 | async-start | bytes 720896 | tf_op jit(solution)/shard_map/all_to_all | solution.py:482
  33.8 0.0 copy-done.3
  33.8 0.7 collective-permute-start
  34.5 0.0 collective-permute-done.edge_hbm.first_edge_hbm
  34.5 13.1 %all-to-all-done.1.sums_ref = f32[16,11,4,128]{3,2,1,0:T(4,128)S(1)} async-done(((f32[16,11,4,128]{3,2,1,0:T(4,128)}), f32[16,11,4,128]{3,2,1,0:T(4,128)S(1)}, u32[]{:S(2)}, u32[]{:S(2)}) %all-to-all-start.1) | async-done | bytes 360480 | tf_op jit(solution)/shard_map/all_to_all | solution.py:482
  47.6 0.0 copy-done
  47.6 0.4 shard_map.107
  48.0 11.6 %all_to_all.25.window_ref = f32[16,8,256]{2,1,0:T(8,128)S(1)} all-to-all(f32[16,8,256]{2,1,0:T(8,128)S(1)} %get-tuple-element.19), channel_id=1, replica_groups=mesh['tm'=32,'lm'=16] {'lm'}, dimensions={0} | all-to-all | bytes 262144 | tf_op jit(solution)/shard_map/all_to_all | solution.py:482
  59.6 0.0 copy-done.1
  59.6 7.8 %shard_map.108 = (f32[16,11,4,128]{3,2,1,0:T(4,128)}, f32[3,8,256]{2,1,0:T(8,128)S(1)}) custom-call(f32[16,8,256]{2,1,0:T(8,128)S(1)} %all_to_all.25.window_ref, s32[8,128]{1,0:T(8,128)S(1)} %copy-done.1, bf16[3,48,64,128]{3,2,1,0:T(8,128)(2,1)S(1)} %shard_map.105.seen_ref), custom_call_target="tpu_custom_call" | custom-call | tf_op jit(solution)/shard_map/pallas_call | solution.py:471
  67.4 3.5 %all-to-all-start.3 = ((f32[16,11,4,128]{3,2,1,0:T(4,128)}), f32[16,11,4,128]{3,2,1,0:T(4,128)S(1)}, u32[]{:S(2)}, u32[]{:S(2)}) async-start(f32[16,11,4,128]{3,2,1,0:T(4,128)} %get-tuple-element.21), calls=%async_computation.3 | async-start | bytes 720896 | tf_op jit(solution)/shard_map/all_to_all | solution.py:482
  70.9 0.7 collective-permute-start.1
  71.5 0.0 collective-permute-done.1.edge_hbm
  71.6 13.0 %all-to-all-done.3.sums_ref = f32[16,11,4,128]{3,2,1,0:T(4,128)S(1)} async-done(((f32[16,11,4,128]{3,2,1,0:T(4,128)}), f32[16,11,4,128]{3,2,1,0:T(4,128)S(1)}, u32[]{:S(2)}, u32[]{:S(2)}) %all-to-all-start.3) | async-done | bytes 360480 | tf_op jit(solution)/shard_map/all_to_all | solution.py:482
  84.6 0.9 shard_map.109
  85.5 3.4 %all-to-all-start.4 = ((f32[16,1,384]{2,1,0:T(1,128)}), f32[16,1,384]{2,1,0:T(1,128)S(1)}, u32[]{:S(2)}, u32[]{:S(2)}) async-start(f32[16,1,384]{2,1,0:T(1,128)} %shard_map.109), calls=%async_computation.4 | async-start | bytes 49152 | tf_op jit(solution)/shard_map/all_to_all | solution.py:482
  88.9 0.8 shard_map.111
  89.8 5.9 %all-to-all-done.4.poses_ref = f32[16,1,384]{2,1,0:T(1,128)S(1)} async-done(((f32[16,1,384]{2,1,0:T(1,128)}), f32[16,1,384]{2,1,0:T(1,128)S(1)}, u32[]{:S(2)}, u32[]{:S(2)}) %all-to-all-start.4) | async-done | bytes 24608 | tf_op jit(solution)/shard_map/all_to_all | solution.py:482
  95.7 0.7 shard_map.110
Async XLA Ops:
  3.2 19.3 %copy-start.2 = (s32[8,128]{1,0:T(8,128)S(1)}, s32[8,128]{1,0:T(8,128)}, u32[]{:S(2)}) copy-start(s32[8,128]{1,0:T(8,128)} %get-tuple-element.14.names_ref) | copy-start | bytes 12292
  3.2 19.3 %all-to-all-start = ((f32[16,8,256]{2,1,0:T(8,128)}), f32[16,8,256]{2,1,0:T(8,128)S(1)}, u32[]{:S(2)}, u32[]{:S(2)}) async-start(f32[16,8,256]{2,1,0:T(8,128)} %get-tuple-element.13), calls=%async_computation | async-start | bytes 262144 | tf_op jit(solution)/shard_map/all_to_all | solution.py:482
  13.4 20.4 %copy-start.3 = (f32[8,256]{1,0:T(8,128)S(1)}, f32[8,256]{1,0:T(8,128)}, u32[]{:S(2)}) copy-start(f32[8,256]{1,0:T(8,128)} %get-tuple-element.18) | copy-start | bytes 24580
  13.4 34.2 %copy-start = (f32[8,256]{1,0:T(8,128)S(1)}, f32[8,256]{1,0:T(8,128)}, u32[]{:S(2)}) copy-start(f32[8,256]{1,0:T(8,128)} %get-tuple-element.17.link_hbm) | copy-start | bytes 24580
  18.7 40.9 %copy-start.1 = (s32[8,128]{1,0:T(8,128)S(1)}, s32[8,128]{1,0:T(8,128)}, u32[]{:S(2)}) copy-start(s32[8,128]{1,0:T(8,128)} %get-tuple-element.20.names_ref) | copy-start | bytes 12292
  30.3 17.2 %all-to-all-start.1 = ((f32[16,11,4,128]{3,2,1,0:T(4,128)}), f32[16,11,4,128]{3,2,1,0:T(4,128)S(1)}, u32[]{:S(2)}, u32[]{:S(2)}) async-start(f32[16,11,4,128]{3,2,1,0:T(4,128)} %get-tuple-element.15), calls=%async_computation.1 | async-start | bytes 720896 | tf_op jit(solution)/shard_map/all_to_all | solution.py:482
  33.8 0.7 collective-permute-start
  67.4 17.2 %all-to-all-start.3 = ((f32[16,11,4,128]{3,2,1,0:T(4,128)}), f32[16,11,4,128]{3,2,1,0:T(4,128)S(1)}, u32[]{:S(2)}, u32[]{:S(2)}) async-start(f32[16,11,4,128]{3,2,1,0:T(4,128)} %get-tuple-element.21), calls=%async_computation.3 | async-start | bytes 720896 | tf_op jit(solution)/shard_map/all_to_all | solution.py:482
  70.9 0.7 collective-permute-start.1
  85.5 10.2 %all-to-all-start.4 = ((f32[16,1,384]{2,1,0:T(1,128)}), f32[16,1,384]{2,1,0:T(1,128)S(1)}, u32[]{:S(2)}, u32[]{:S(2)}) async-start(f32[16,1,384]{2,1,0:T(1,128)} %shard_map.109), calls=%async_computation.4 | async-start | bytes 49152 | tf_op jit(solution)/shard_map/all_to_all | solution.py:482

commit v4 on v3

--- a/solution.py
+++ b/solution.py
@@ -25,6 +25,11 @@
 
 def half_turn(x):
     return pltpu.roll(x, 64, 1)
+
+
+def own_frames():
+    owners = lax.axis_size("lm")
+    return lax.rem(lax.axis_index("lm") + owners // 2 - 1, owners)
 
 
 def own_block(ref, block):
@@ -91,12 +96,12 @@
     for load in loads:
         load.start()
     rows[...] = jnp.zeros((8, 1024), jnp.float32)
-    owner = lax.axis_index("lm")
+    block_of_frames = own_frames()
     lane = lanes((8, 128))
     for load in loads:
         load.wait()
     rows[0:6, :] = poses[...]
-    pose = own_block(rows, owner)
+    pose = own_block(rows, block_of_frames)
     for k in range(3):
         for b in range(8):
             chunk[b : b + 1, k * 64 : (k + 1) * 64] = points[k : k + 1, b * 64 : (b + 1) * 64]
@@ -107,8 +112,8 @@
         send.start()
     rows[0:6, :] = odometry[...]
     rows[6:7, :] = info[...]
-    current = own_block(rows, owner)
-    before = own_block(rows, owner - 1)
+    current = own_block(rows, block_of_frames)
+    before = own_block(rows, block_of_frames - 1)
     edge[:, 0:128] = pose
     edge[:, 128:256] = current
     sends.append(pltpu.make_async_copy(edge, edge_hbm, sems.at[7]))
@@ -124,7 +129,7 @@
     position = dot(table, named)[0:1].astype(jnp.int32)
     live = lanes((1, slots)) < count_ref[0]
     names_ref[...] = jnp.full(names_ref.shape, -1, jnp.int32)
-    names_ref[0:1, 0:slots] = jnp.where(live, frame[...], -1)
+    names_ref[0:1, 0:slots] = jnp.where(live, (frame[...] + owners // 2 + 1) & (owners - 1), -1)
     names_ref[1:2, 0:slots] = jnp.where(live, position, -1)
     for n in range(2):
         name = names_ref[...][n : n + 1]
@@ -191,8 +196,8 @@
     near_ref, pose, point, fsum, psum, partial, right, sums, sems = scratch
     owner, owners = lax.axis_index("lm"), lax.axis_size("lm")
     near_ref[0] = window_ref[owner]
-    near_ref[1] = window_ref[jnp.maximum(owner - 1, 0)]
-    near_ref[2] = window_ref[jnp.minimum(owner + 1, owners - 1)]
+    near_ref[1] = window_ref[lax.rem(owner + owners - 1, owners)]
+    near_ref[2] = window_ref[lax.rem(owner + 1, owners)]
     turned = split(jnp.transpose(window_ref[...].reshape(128, 256), (1, 0)), PARTS)
     put_near = pltpu.make_async_copy(near_ref, near_hbm, sems.at[7])
     put_near.start()
@@ -347,12 +352,12 @@
 
 
 def new_poses(lower_sums, upper_sums, near_ref, link_ref, edge_ref, first_edge_ref, scratch):
-    owner, shard = lax.axis_index("lm"), lax.axis_index("tm")
+    block, shard = own_frames(), lax.axis_index("tm")
     owners, shards = lax.axis_size("lm"), lax.axis_size("tm")
     lane = lanes((8, 128))
     current, before, after = (half_turn(near_ref[n, :, 128:256]) for n in range(3))
     outside = edge_ref[:, 0:128]
-    initial, final = owner == 0, owner == owners - 1
+    initial, final = block == 0, block == owners - 1
     before = jnp.where(initial, outside, before)
     after = jnp.where(final, outside, after)
     previous = jnp.where(lane == 0, pltpu.roll(before, 65, 1), pltpu.roll(current, 1, 1))
@@ -448,21 +453,20 @@
             copies_ref[d, :, h * 128 : (h + 1) * 128] = pair
 
 
-def last_points_kernel(sums_ref, near_hbm, out_ref, near_ref, sem):
+def last_kernel(copies_ref, sums_ref, near_hbm, poses_ref, points_ref, near_ref, sem):
     load = pltpu.make_async_copy(near_hbm, near_ref, sem)
     load.start()
+    owners = copies_ref.shape[0]
+    for d in range(owners):
+        block = (d + owners // 2 - 1) % owners
+        for k in range(6):
+            poses_ref[k : k + 1, block * 64 : (block + 1) * 64] = copies_ref[d, :, k * 64 : (k + 1) * 64]
     sums = [pair_total(sums_ref, k) for k in range(5)]
     load.wait()
     x = new_points(sums, near_ref)
     for k in range(3):
         for b in range(8):
-            out_ref[k : k + 1, b * 64 : (b + 1) * 64] = x[k][b : b + 1, 0:64]
-
-
-def spread_kernel(poses_ref, out_ref):
-    for d in range(poses_ref.shape[0]):
-        for k in range(6):
-            out_ref[k : k + 1, d * 64 : (d + 1) * 64] = poses_ref[d, :, k * 64 : (k + 1) * 64]
+            points_ref[k : k + 1, b * 64 : (b + 1) * 64] = x[k][b : b + 1, 0:64]
 
 
 def call(kernel, outs, scratch, args, spaces, room=48):
@@ -499,8 +503,8 @@
     seen = jnp.transpose(observations, (1, 2, 3, 0))
     to_edges = []
     for a in range(shards - 1):
-        to_edges.append((a * owners + owners - 1, (a + 1) * owners))
-        to_edges.append(((a + 1) * owners, a * owners + owners - 1))
+        end, start = a * owners + owners // 2, (a + 1) * owners + owners // 2 + 1
+        to_edges += [(end, start), (start, end)]
 
     def edges(array):
         return lax.ppermute(array, ("tm", "lm"), to_edges)
@@ -594,11 +598,13 @@
         [sums, near, link, edge, first_edge],
         "vhhhhv",
     )
-    gathered = exchange(copies)
-    (points,) = call(
-        last_points_kernel, [shape(*landmarks.shape)], [buffer(3, 8, 256), dma], [sums, near], "vhv"
+    poses, points = call(
+        last_kernel,
+        [shape(*camera_poses.shape), shape(*landmarks.shape)],
+        [buffer(3, 8, 256), dma],
+        [exchange(copies), sums, near],
+        "vvhvv",
     )
-    (poses,) = call(spread_kernel, [shape(*camera_poses.shape)], [], [gathered], "vv")
     return (poses, points)
 
 

time: 97 us -> 96.3 us (level)
  blocking collectives: 11.6 us -> 21.5 us
  waiting for transfers between devices: 35.8 us -> 29.9 us
  starting transfers between devices: 21.8 us -> 18.4 us
  Pallas kernels: 25.8 us -> 24.5 us
    all_to_all x1 -> x2, blocking collectives: 11.6 us -> 21.5 us  [exchange(): return lax.all_to_all(array, 'lm', 0, 0, tiled=True)]
    all_to_all x4 -> x3, waiting for transfers between devices: 35.8 us -> 29.9 us  [exchange(): return lax.all_to_all(array, 'lm', 0, 0, tiled=True)]
    all_to_all x4 -> x3, starting transfers between devices: 20.5 us -> 17.1 us  [exchange(): return lax.all_to_all(array, 'lm', 0, 0, tiled=True)]
    pallas_call x8 -> x7, Pallas kernels: 25.8 us -> 24.5 us  [call(): pl.pallas_call(kernel, out_shape=outs, in_specs=specs[:len(args)], out_sp...]
  transfers between devices with their start and end apart: 6 -> 5, of which waited for: 4 -> 3; matrix products, arithmetic and copies ran while one was open for 0% -> 0% of each run, Pallas kernels for 6% -> 6%
where the time goes in v4:
time: 96.3 us; the launch traced here: 95.8 us
  waiting for transfers between devices  29.9 us (31%)
  Pallas kernels  24.5 us (25%)
  blocking collectives  21.5 us (22%)
  starting transfers between devices  18.4 us (19%)
  between operations  1.4 us (1%)
    all_to_all x3, waiting for transfers between devices, exchange(): return lax.all_to_all(array, 'lm', 0, 0, tiled=True)  29.9 us
    pallas_call x7, Pallas kernels, call(): pl.pallas_call(kernel, out_shape=outs, in_specs=specs[:len(args)], out_sp...  24.5 us
    all_to_all x2, blocking collectives, exchange(): return lax.all_to_all(array, 'lm', 0, 0, tiled=True)  21.5 us
    all_to_all x3, starting transfers between devices, exchange(): return lax.all_to_all(array, 'lm', 0, 0, tiled=True)  17.1 us
  transfers between devices with their start and end apart: 5, of which 3 were waited for; matrix products, arithmetic and copies ran while one was open for 0% of the time, Pallas kernels for 6%

profile of v4, /device:TPU:1, one launch (start us, length us, event | category | flops | bytes accessed | tf_op | source)
XLA Modules:
  0.0 95.8 jit_solution(270351936412153104)
XLA Ops:
  1.3 1.9 %shard_map.104 = (f32[16,8,256]{2,1,0:T(8,128)}, f32[8,256]{1,0:T(8,128)}, f32[8,256]{1,0:T(8,128)}, s32[8,128]{1,0:T(8,128)}, s32[8,128]{1,0:T(8,128)}) custom-call(s32[1]{0:T(128)S(6)} %copy.11.count_ref, f32[3,512]{1,0:T(4,128)} %points_hbm.1, f32[6,1024]{1,0:T(8,128)} %poses_hbm.1, f32[6,1024]{1,0:T(8,128)} %odometry_hbm.1, f32[1,1024]{1,0:T(1,128)} %bitcast.5, ...), custom_call_target="tpu_custom_call" | custom-call | tf_op jit(solution)/shard_map/pallas_call | solution.py:475
  3.2 0.0 copy-start.2
  3.2 10.1 %all-to-all-start = ((f32[16,8,256]{2,1,0:T(8,128)}), f32[16,8,256]{2,1,0:T(8,128)S(1)}, u32[]{:S(2)}, u32[]{:S(2)}) async-start(f32[16,8,256]{2,1,0:T(8,128)} %get-tuple-element.13), calls=%async_computation | async-start | bytes 262144 | tf_op jit(solution)/shard_map/all_to_all | solution.py:486
  13.4 0.0 copy-start.3
  13.4 0.0 copy-start
  13.4 5.3 %shard_map.105.seen_ref = bf16[3,48,64,128]{3,2,1,0:T(8,128)(2,1)S(1)} custom-call(bf16[3,64,64,96]{3,2,1,0:T(8,128)(2,1)} %bitcast.4), custom_call_target="tpu_custom_call" | custom-call | tf_op jit(solution)/shard_map/pallas_call | solution.py:475
  18.7 0.0 copy-start.1
  18.7 3.8 %all-to-all-done.window_ref = f32[16,8,256]{2,1,0:T(8,128)S(1)} async-done(((f32[16,8,256]{2,1,0:T(8,128)}), f32[16,8,256]{2,1,0:T(8,128)S(1)}, u32[]{:S(2)}, u32[]{:S(2)}) %all-to-all-start) | async-done | bytes 131104 | tf_op jit(solution)/shard_map/all_to_all | solution.py:486
  22.6 0.0 copy-done.2
  22.6 7.8 %shard_map.106 = (f32[16,11,4,128]{3,2,1,0:T(4,128)}, f32[3,8,256]{2,1,0:T(8,128)S(1)}) custom-call(f32[16,8,256]{2,1,0:T(8,128)S(1)} %all-to-all-done.window_ref, s32[8,128]{1,0:T(8,128)S(1)} %copy-done.2, bf16[3,48,64,128]{3,2,1,0:T(8,128)(2,1)S(1)} %shard_map.105.seen_ref), custom_call_target="tpu_custom_call" | custom-call | tf_op jit(solution)/shard_map/pallas_call | solution.py:475
  30.4 3.5 %all-to-all-start.1 = ((f32[16,11,4,128]{3,2,1,0:T(4,128)}), f32[16,11,4,128]{3,2,1,0:T(4,128)S(1)}, u32[]{:S(2)}, u32[]{:S(2)}) async-start(f32[16,11,4,128]{3,2,1,0:T(4,128)} %get-tuple-element.15), calls=%async_computation.1 | async-start | bytes 720896 | tf_op jit(solution)/shard_map/all_to_all | solution.py:486
  33.8 0.0 copy-done.3
  33.8 0.7 collective-permute-start
  34.5 0.0 collective-permute-done.edge_hbm.first_edge_hbm
  34.5 13.1 %all-to-all-done.1.sums_ref = f32[16,11,4,128]{3,2,1,0:T(4,128)S(1)} async-done(((f32[16,11,4,128]{3,2,1,0:T(4,128)}), f32[16,11,4,128]{3,2,1,0:T(4,128)S(1)}, u32[]{:S(2)}, u32[]{:S(2)}) %all-to-all-start.1) | async-done | bytes 360480 | tf_op jit(solution)/shard_map/all_to_all | solution.py:486
  47.6 0.0 copy-done
  47.6 0.4 shard_map.107
  48.0 11.6 %all_to_all.25.window_ref = f32[16,8,256]{2,1,0:T(8,128)S(1)} all-to-all(f32[16,8,256]{2,1,0:T(8,128)S(1)} %get-tuple-element.19), channel_id=1, replica_groups=mesh['tm'=32,'lm'=16] {'lm'}, dimensions={0} | all-to-all | bytes 262144 | tf_op jit(solution)/shard_map/all_to_all | solution.py:486
  59.6 0.0 copy-done.1
  59.6 7.8 %shard_map.108 = (f32[16,11,4,128]{3,2,1,0:T(4,128)}, f32[3,8,256]{2,1,0:T(8,128)S(1)}) custom-call(f32[16,8,256]{2,1,0:T(8,128)S(1)} %all_to_all.25.window_ref, s32[8,128]{1,0:T(8,128)S(1)} %copy-done.1, bf16[3,48,64,128]{3,2,1,0:T(8,128)(2,1)S(1)} %shard_map.105.seen_ref), custom_call_target="tpu_custom_call" | custom-call | tf_op jit(solution)/shard_map/pallas_call | solution.py:475
  67.4 3.5 %all-to-all-start.3 = ((f32[16,11,4,128]{3,2,1,0:T(4,128)}), f32[16,11,4,128]{3,2,1,0:T(4,128)S(1)}, u32[]{:S(2)}, u32[]{:S(2)}) async-start(f32[16,11,4,128]{3,2,1,0:T(4,128)} %get-tuple-element.21), calls=%async_computation.3 | async-start | bytes 720896 | tf_op jit(solution)/shard_map/all_to_all | solution.py:486
  70.9 0.7 collective-permute-start.1
  71.5 0.0 collective-permute-done.1.edge_hbm
  71.6 13.0 %all-to-all-done.3.sums_ref = f32[16,11,4,128]{3,2,1,0:T(4,128)S(1)} async-done(((f32[16,11,4,128]{3,2,1,0:T(4,128)}), f32[16,11,4,128]{3,2,1,0:T(4,128)S(1)}, u32[]{:S(2)}, u32[]{:S(2)}) %all-to-all-start.3) | async-done | bytes 360480 | tf_op jit(solution)/shard_map/all_to_all | solution.py:486
  84.6 0.3 shard_map.109
  84.9 9.9 %all_to_all.26.copies_ref = f32[16,1,384]{2,1,0:T(1,128)S(1)} all-to-all(f32[16,1,384]{2,1,0:T(1,128)S(1)} %shard_map.109), channel_id=1, replica_groups=mesh['tm'=32,'lm'=16] {'lm'}, dimensions={0} | all-to-all | bytes 49152 | tf_op jit(solution)/shard_map/all_to_all | solution.py:486
  94.9 0.9 shard_map.110
Async XLA Ops:
  3.2 19.3 %copy-start.2 = (s32[8,128]{1,0:T(8,128)S(1)}, s32[8,128]{1,0:T(8,128)}, u32[]{:S(2)}) copy-start(s32[8,128]{1,0:T(8,128)} %get-tuple-element.14.names_ref) | copy-start | bytes 12292
  3.2 19.3 %all-to-all-start = ((f32[16,8,256]{2,1,0:T(8,128)}), f32[16,8,256]{2,1,0:T(8,128)S(1)}, u32[]{:S(2)}, u32[]{:S(2)}) async-start(f32[16,8,256]{2,1,0:T(8,128)} %get-tuple-element.13), calls=%async_computation | async-start | bytes 262144 | tf_op jit(solution)/shard_map/all_to_all | solution.py:486
  13.4 20.4 %copy-start.3 = (f32[8,256]{1,0:T(8,128)S(1)}, f32[8,256]{1,0:T(8,128)}, u32[]{:S(2)}) copy-start(f32[8,256]{1,0:T(8,128)} %get-tuple-element.18) | copy-start | bytes 24580
  13.4 34.2 %copy-start = (f32[8,256]{1,0:T(8,128)S(1)}, f32[8,256]{1,0:T(8,128)}, u32[]{:S(2)}) copy-start(f32[8,256]{1,0:T(8,128)} %get-tuple-element.17.link_hbm) | copy-start | bytes 24580
  18.7 40.9 %copy-start.1 = (s32[8,128]{1,0:T(8,128)S(1)}, s32[8,128]{1,0:T(8,128)}, u32[]{:S(2)}) copy-start(s32[8,128]{1,0:T(8,128)} %get-tuple-element.20.names_ref) | copy-start | bytes 12292
  30.4 17.2 %all-to-all-start.1 = ((f32[16,11,4,128]{3,2,1,0:T(4,128)}), f32[16,11,4,128]{3,2,1,0:T(4,128)S(1)}, u32[]{:S(2)}, u32[]{:S(2)}) async-start(f32[16,11,4,128]{3,2,1,0:T(4,128)} %get-tuple-element.15), calls=%async_computation.1 | async-start | bytes 720896 | tf_op jit(solution)/shard_map/all_to_all | solution.py:486
  33.8 0.7 collective-permute-start
  67.4 17.2 %all-to-all-start.3 = ((f32[16,11,4,128]{3,2,1,0:T(4,128)}), f32[16,11,4,128]{3,2,1,0:T(4,128)S(1)}, u32[]{:S(2)}, u32[]{:S(2)}) async-start(f32[16,11,4,128]{3,2,1,0:T(4,128)} %get-tuple-element.21), calls=%async_computation.3 | async-start | bytes 720896 | tf_op jit(solution)/shard_map/all_to_all | solution.py:486
  70.9 0.7 collective-permute-start.1

commit v5 on v4

--- a/solution.py
+++ b/solution.py
@@ -164,23 +164,26 @@
 def fold_kernel(seen_hbm, folded, seen, sems):
     parts = [pl.ds(PLAIN, FOLDED)] + [pl.ds(g * FOLDED, FOLDED) for g in range(GROUPS)]
     loads = [
-        pltpu.make_async_copy(seen_hbm.at[:, part], seen.at[:, part], sems.at[n]) for n, part in enumerate(parts)
+        pltpu.make_async_copy(seen_hbm.at[k, part], seen.at[k, part], sems.at[n, k])
+        for n, part in enumerate(parts)
+        for k in range(3)
     ]
     for load in loads:
         load.start()
-    loads[0].wait()
     for g in range(GROUPS):
-        loads[1 + g].wait()
-
-        def step(m, carry):
-            for k in range(3):
+        for k in range(3):
+            if g == 0:
+                loads[k].wait()
+            loads[3 + g * 3 + k].wait()
+
+            def step(m, carry):
                 for r in range(0, TILE, 16):
                     wide = seen[k, g * FOLDED + m, r : r + 16, :]
                     more = seen[k, PLAIN + m, r : r + 16, g * EXTRA : (g + 1) * EXTRA]
                     folded[k, g * FOLDED + m, r : r + 16, :] = jnp.concatenate([wide, more], axis=1)
-            return carry
-
-        lax.fori_loop(0, FOLDED, step, 0)
+                return carry
+
+            lax.fori_loop(0, FOLDED, step, 0, unroll=4)
 
 
 def unfold(parts):
@@ -192,33 +195,44 @@
     return result
 
 
-def tiles_kernel(window_ref, names_ref, seen_ref, out_hbm, near_hbm, *scratch):
-    near_ref, pose, point, fsum, psum, partial, right, sums, sems = scratch
-    owner, owners = lax.axis_index("lm"), lax.axis_size("lm")
-    near_ref[0] = window_ref[owner]
-    near_ref[1] = window_ref[lax.rem(owner + owners - 1, owners)]
-    near_ref[2] = window_ref[lax.rem(owner + 1, owners)]
-    turned = split(jnp.transpose(window_ref[...].reshape(128, 256), (1, 0)), PARTS)
-    put_near = pltpu.make_async_copy(near_ref, near_hbm, sems.at[7])
-    put_near.start()
+def pick_poses(turned, names_ref, pose):
     row = lax.broadcasted_iota(jnp.int32, (128, 128), 0)
     lane = lanes((FOLDED, 128))
-    points = jnp.concatenate([piece[0:192] for piece in turned], axis=0)
     for g in range(GROUPS):
-        frame, position = names_ref[2 + g : 3 + g, :], names_ref[2 + GROUPS + g : 3 + GROUPS + g, :]
-        pick = jnp.where(position == row, 1.0, 0.0).astype(jnp.bfloat16)
-        found = dot(points, pick)
-        point[g * 192 : (g + 1) * 192, :] = sum(found[n * 192 : (n + 1) * 192] for n in range(PARTS))
-        at = 192 + g * FOLDED
-        poses = jnp.concatenate(
-            [piece[r : r + FOLDED] for r in (at, 192 + PLAIN) for piece in turned], axis=0
-        )
+        frame = names_ref[2 + g : 3 + g, :]
+        at = g * FOLDED
+        poses = jnp.concatenate([piece[r : r + FOLDED] for r in (at, PLAIN) for piece in turned], axis=0)
         for k in range(6):
             pick = jnp.where(frame * 8 + k == row, 1.0, 0.0).astype(jnp.bfloat16)
             both = dot(poses, pick)
             found = [both[n * FOLDED : (n + 1) * FOLDED] for n in range(2 * PARTS)]
             found = [sum(found[:PARTS]), sum(found[PARTS:])]
-            pose[k * PLAIN + g * FOLDED : k * PLAIN + (g + 1) * FOLDED, :] = jnp.where(lane < SLOTS, *found)
+            pose[k * PLAIN + at : k * PLAIN + at + FOLDED, :] = jnp.where(lane < SLOTS, *found)
+
+
+def tiles_kernel(window_ref, names_ref, seen_ref, out_hbm, near_hbm, near_ref, pose, sem, *scratch):
+    owner, owners = lax.axis_index("lm"), lax.axis_size("lm")
+    near_ref[0] = window_ref[owner]
+    near_ref[1] = window_ref[lax.rem(owner + owners - 1, owners)]
+    near_ref[2] = window_ref[lax.rem(owner + 1, owners)]
+    put_near = pltpu.make_async_copy(near_ref, near_hbm, sem)
+    put_near.start()
+    turned = split(jnp.transpose(window_ref[...].reshape(128, 256), (1, 0)), PARTS)
+    pick_poses([piece[192:256] for piece in turned], names_ref, pose)
+    points = [piece[0:192] for piece in turned]
+    add_tiles(points, names_ref, seen_ref, pose, out_hbm, *scratch)
+    put_near.wait()
+
+
+def add_tiles(points, names_ref, seen_ref, pose, out_hbm, point, fsum, psum, partial, right, sums, sems):
+    row = lax.broadcasted_iota(jnp.int32, (128, 128), 0)
+    lane = lanes((FOLDED, 128))
+    points = jnp.concatenate(points, axis=0)
+    for g in range(GROUPS):
+        position = names_ref[2 + GROUPS + g : 3 + GROUPS + g, :]
+        pick = jnp.where(position == row, 1.0, 0.0).astype(jnp.bfloat16)
+        found = dot(points, pick)
+        point[g * 192 : (g + 1) * 192, :] = sum(found[n * 192 : (n + 1) * 192] for n in range(PARTS))
     psum[...] = jnp.zeros_like(psum)
     partial[...] = jnp.zeros_like(partial)
 
@@ -314,7 +328,6 @@
         right[:, 2 * r, :] = half_turn(pair)
         right[:, 2 * r + 1, :] = pair
         sums[:, 10, r, :] = frames[:, (4 + r) * 128 : (5 + r) * 128]
-    put_near.wait()
     stores = [pltpu.make_async_copy(sums.at[:, 10], out_hbm.at[:, 10], sems.at[5])]
     stores[0].start()
     own = jnp.where(held, scale, 0.0).astype(jnp.bfloat16)
@@ -553,7 +566,7 @@
         [jax.ShapeDtypeStruct((3, PLAIN, TILE, 128), seen.dtype)],
         [
             pltpu.VMEM(seen.shape, seen.dtype),
-            dma((1 + GROUPS,)),
+            dma((1 + GROUPS, 3)),
         ],
         [seen],
         "hv",
@@ -569,13 +582,14 @@
             [
                 buffer(3, 8, 256),
                 buffer(6 * PLAIN, 128),
+                dma,
                 buffer(GROUPS * 192, 128),
                 buffer(16 * PLAIN, 128),
                 buffer(GROUPS, 576, 128),
                 buffer(128, 128),
                 buffer(owners, 8, 128),
                 buffer(owners, 11, 4, 128),
-                dma((8,)),
+                dma((6,)),
             ],
             [window, names[iteration], folded],
             "vvvhh",

time: 96.3 us -> 95.2 us (0.989)
  Pallas kernels: 24.5 us -> 22.9 us
    pallas_call x7, Pallas kernels: 24.5 us -> 22.9 us  [call(): pl.pallas_call(kernel, out_shape=outs, in_specs=specs[:len(args)], out_sp...]
  transfers between devices with their start and end apart: 5 -> 5, of which waited for: 3 -> 3; matrix products, arithmetic and copies ran while one was open for 0% -> 0% of each run, Pallas kernels for 6% -> 5%
where the time goes in v5:
time: 95.2 us; the launch traced here: 94.7 us
  waiting for transfers between devices  30.3 us (32%)
  Pallas kernels  22.9 us (24%)
  blocking collectives  21.6 us (23%)
  starting transfers between devices  18.4 us (19%)
  between operations  1.42 us (1%)
    all_to_all x3, waiting for transfers between devices, exchange(): return lax.all_to_all(array, 'lm', 0, 0, tiled=True)  30.3 us
    pallas_call x7, Pallas kernels, call(): pl.pallas_call(kernel, out_shape=outs, in_specs=specs[:len(args)], out_sp...  22.9 us
    all_to_all x2, blocking collectives, exchange(): return lax.all_to_all(array, 'lm', 0, 0, tiled=True)  21.6 us
    all_to_all x3, starting transfers between devices, exchange(): return lax.all_to_all(array, 'lm', 0, 0, tiled=True)  17.1 us
  transfers between devices with their start and end apart: 5, of which 3 were waited for; matrix products, arithmetic and copies ran while one was open for 0% of the time, Pallas kernels for 5%

profile of v5, /device:TPU:1, one launch (start us, length us, event | category | flops | bytes accessed | tf_op | source)
XLA Modules:
  0.0 94.7 jit_solution(5236628381936231713)
XLA Ops:
  1.3 1.9 %shard_map.104 = (f32[16,8,256]{2,1,0:T(8,128)}, f32[8,256]{1,0:T(8,128)}, f32[8,256]{1,0:T(8,128)}, s32[8,128]{1,0:T(8,128)}, s32[8,128]{1,0:T(8,128)}) custom-call(s32[1]{0:T(128)S(6)} %copy.11.count_ref, f32[3,512]{1,0:T(4,128)} %points_hbm.1, f32[6,1024]{1,0:T(8,128)} %poses_hbm.1, f32[6,1024]{1,0:T(8,128)} %odometry_hbm.1, f32[1,1024]{1,0:T(1,128)} %bitcast.5, ...), custom_call_target="tpu_custom_call" | custom-call | tf_op jit(solution)/shard_map/pallas_call | solution.py:488
  3.2 0.0 copy-start.2
  3.2 10.1 %all-to-all-start = ((f32[16,8,256]{2,1,0:T(8,128)}), f32[16,8,256]{2,1,0:T(8,128)S(1)}, u32[]{:S(2)}, u32[]{:S(2)}) async-start(f32[16,8,256]{2,1,0:T(8,128)} %get-tuple-element.13), calls=%async_computation | async-start | bytes 262144 | tf_op jit(solution)/shard_map/all_to_all | solution.py:499
  13.4 0.0 copy-start.3
  13.4 0.0 copy-start
  13.4 4.4 %shard_map.105.seen_ref = bf16[3,48,64,128]{3,2,1,0:T(8,128)(2,1)S(1)} custom-call(bf16[3,64,64,96]{3,2,1,0:T(8,128)(2,1)} %bitcast.4), custom_call_target="tpu_custom_call" | custom-call | tf_op jit(solution)/shard_map/pallas_call | solution.py:488
  17.8 0.0 copy-start.1
  17.8 4.8 %all-to-all-done.window_ref = f32[16,8,256]{2,1,0:T(8,128)S(1)} async-done(((f32[16,8,256]{2,1,0:T(8,128)}), f32[16,8,256]{2,1,0:T(8,128)S(1)}, u32[]{:S(2)}, u32[]{:S(2)}) %all-to-all-start) | async-done | bytes 131104 | tf_op jit(solution)/shard_map/all_to_all | solution.py:499
  22.6 0.0 copy-done.2
  22.6 7.4 %shard_map.106 = (f32[16,11,4,128]{3,2,1,0:T(4,128)}, f32[3,8,256]{2,1,0:T(8,128)S(1)}) custom-call(f32[16,8,256]{2,1,0:T(8,128)S(1)} %all-to-all-done.window_ref, s32[8,128]{1,0:T(8,128)S(1)} %copy-done.2, bf16[3,48,64,128]{3,2,1,0:T(8,128)(2,1)S(1)} %shard_map.105.seen_ref), custom_call_target="tpu_custom_call" | custom-call | tf_op jit(solution)/shard_map/pallas_call | solution.py:488
  30.0 3.5 %all-to-all-start.1 = ((f32[16,11,4,128]{3,2,1,0:T(4,128)}), f32[16,11,4,128]{3,2,1,0:T(4,128)S(1)}, u32[]{:S(2)}, u32[]{:S(2)}) async-start(f32[16,11,4,128]{3,2,1,0:T(4,128)} %get-tuple-element.15), calls=%async_computation.1 | async-start | bytes 720896 | tf_op jit(solution)/shard_map/all_to_all | solution.py:499
  33.5 0.0 copy-done.3
  33.5 0.7 collective-permute-start
  34.2 0.0 collective-permute-done.edge_hbm.first_edge_hbm
  34.2 12.6 %all-to-all-done.1.sums_ref = f32[16,11,4,128]{3,2,1,0:T(4,128)S(1)} async-done(((f32[16,11,4,128]{3,2,1,0:T(4,128)}), f32[16,11,4,128]{3,2,1,0:T(4,128)S(1)}, u32[]{:S(2)}, u32[]{:S(2)}) %all-to-all-start.1) | async-done | bytes 360480 | tf_op jit(solution)/shard_map/all_to_all | solution.py:499
  46.7 0.0 copy-done
  46.7 0.4 shard_map.107
  47.2 11.7 %all_to_all.25.window_ref = f32[16,8,256]{2,1,0:T(8,128)S(1)} all-to-all(f32[16,8,256]{2,1,0:T(8,128)S(1)} %get-tuple-element.19), channel_id=1, replica_groups=mesh['tm'=32,'lm'=16] {'lm'}, dimensions={0} | all-to-all | bytes 262144 | tf_op jit(solution)/shard_map/all_to_all | solution.py:499
  58.9 0.0 copy-done.1
  58.9 7.4 %shard_map.108 = (f32[16,11,4,128]{3,2,1,0:T(4,128)}, f32[3,8,256]{2,1,0:T(8,128)S(1)}) custom-call(f32[16,8,256]{2,1,0:T(8,128)S(1)} %all_to_all.25.window_ref, s32[8,128]{1,0:T(8,128)S(1)} %copy-done.1, bf16[3,48,64,128]{3,2,1,0:T(8,128)(2,1)S(1)} %shard_map.105.seen_ref), custom_call_target="tpu_custom_call" | custom-call | tf_op jit(solution)/shard_map/pallas_call | solution.py:488
  66.3 3.5 %all-to-all-start.3 = ((f32[16,11,4,128]{3,2,1,0:T(4,128)}), f32[16,11,4,128]{3,2,1,0:T(4,128)S(1)}, u32[]{:S(2)}, u32[]{:S(2)}) async-start(f32[16,11,4,128]{3,2,1,0:T(4,128)} %get-tuple-element.21), calls=%async_computation.3 | async-start | bytes 720896 | tf_op jit(solution)/shard_map/all_to_all | solution.py:499
  69.8 0.7 collective-permute-start.1
  70.5 0.0 collective-permute-done.1.edge_hbm
  70.5 13.0 %all-to-all-done.3.sums_ref = f32[16,11,4,128]{3,2,1,0:T(4,128)S(1)} async-done(((f32[16,11,4,128]{3,2,1,0:T(4,128)}), f32[16,11,4,128]{3,2,1,0:T(4,128)S(1)}, u32[]{:S(2)}, u32[]{:S(2)}) %all-to-all-start.3) | async-done | bytes 360480 | tf_op jit(solution)/shard_map/all_to_all | solution.py:499
  83.5 0.3 shard_map.109
  83.8 9.9 %all_to_all.26.copies_ref = f32[16,1,384]{2,1,0:T(1,128)S(1)} all-to-all(f32[16,1,384]{2,1,0:T(1,128)S(1)} %shard_map.109), channel_id=1, replica_groups=mesh['tm'=32,'lm'=16] {'lm'}, dimensions={0} | all-to-all | bytes 49152 | tf_op jit(solution)/shard_map/all_to_all | solution.py:499
  93.8 0.9 shard_map.110
Async XLA Ops:
  3.2 19.3 %copy-start.2 = (s32[8,128]{1,0:T(8,128)S(1)}, s32[8,128]{1,0:T(8,128)}, u32[]{:S(2)}) copy-start(s32[8,128]{1,0:T(8,128)} %get-tuple-element.14.names_ref) | copy-start | bytes 12292
  3.2 19.3 %all-to-all-start = ((f32[16,8,256]{2,1,0:T(8,128)}), f32[16,8,256]{2,1,0:T(8,128)S(1)}, u32[]{:S(2)}, u32[]{:S(2)}) async-start(f32[16,8,256]{2,1,0:T(8,128)} %get-tuple-element.13), calls=%async_computation | async-start | bytes 262144 | tf_op jit(solution)/shard_map/all_to_all | solution.py:499
  13.4 20.1 %copy-start.3 = (f32[8,256]{1,0:T(8,128)S(1)}, f32[8,256]{1,0:T(8,128)}, u32[]{:S(2)}) copy-start(f32[8,256]{1,0:T(8,128)} %get-tuple-element.18) | copy-start | bytes 24580
  13.4 33.3 %copy-start = (f32[8,256]{1,0:T(8,128)S(1)}, f32[8,256]{1,0:T(8,128)}, u32[]{:S(2)}) copy-start(f32[8,256]{1,0:T(8,128)} %get-tuple-element.17.link_hbm) | copy-start | bytes 24580
  17.8 41.1 %copy-start.1 = (s32[8,128]{1,0:T(8,128)S(1)}, s32[8,128]{1,0:T(8,128)}, u32[]{:S(2)}) copy-start(s32[8,128]{1,0:T(8,128)} %get-tuple-element.20.names_ref) | copy-start | bytes 12292
  30.0 16.7 %all-to-all-start.1 = ((f32[16,11,4,128]{3,2,1,0:T(4,128)}), f32[16,11,4,128]{3,2,1,0:T(4,128)S(1)}, u32[]{:S(2)}, u32[]{:S(2)}) async-start(f32[16,11,4,128]{3,2,1,0:T(4,128)} %get-tuple-element.15), calls=%async_computation.1 | async-start | bytes 720896 | tf_op jit(solution)/shard_map/all_to_all | solution.py:499
  33.5 0.7 collective-permute-start
  66.3 17.2 %all-to-all-start.3 = ((f32[16,11,4,128]{3,2,1,0:T(4,128)}), f32[16,11,4,128]{3,2,1,0:T(4,128)S(1)}, u32[]{:S(2)}, u32[]{:S(2)}) async-start(f32[16,11,4,128]{3,2,1,0:T(4,128)} %get-tuple-element.21), calls=%async_computation.3 | async-start | bytes 720896 | tf_op jit(solution)/shard_map/all_to_all | solution.py:499
  69.8 0.7 collective-permute-start.1

commit v6 on v5

--- a/solution.py
+++ b/solution.py
@@ -98,8 +98,7 @@
     rows[...] = jnp.zeros((8, 1024), jnp.float32)
     block_of_frames = own_frames()
     lane = lanes((8, 128))
-    for load in loads:
-        load.wait()
+    wait_all(loads[:2])
     rows[0:6, :] = poses[...]
     pose = own_block(rows, block_of_frames)
     for k in range(3):
@@ -110,6 +109,7 @@
     sends = [pltpu.make_async_copy(chunk, copies_hbm.at[d], sems.at[10 + d]) for d in range(owners)]
     for send in sends:
         send.start()
+    wait_all(loads[2:])
     rows[0:6, :] = odometry[...]
     rows[6:7, :] = info[...]
     current = own_block(rows, block_of_frames)

time: 95.2 us -> 95.4 us (level)
  no operation moved by 1% of the time
where the time goes in v6:
time: 95.4 us; the launch traced here: 94.8 us
  waiting for transfers between devices  30.3 us (32%)
  Pallas kernels  23 us (24%)
  blocking collectives  21.6 us (23%)
  starting transfers between devices  18.4 us (19%)
  between operations  1.42 us (1%)
    all_to_all x3, waiting for transfers between devices, exchange(): return lax.all_to_all(array, 'lm', 0, 0, tiled=True)  30.3 us
    pallas_call x7, Pallas kernels, call(): pl.pallas_call(kernel, out_shape=outs, in_specs=specs[:len(args)], out_sp...  23 us
    all_to_all x2, blocking collectives, exchange(): return lax.all_to_all(array, 'lm', 0, 0, tiled=True)  21.6 us
    all_to_all x3, starting transfers between devices, exchange(): return lax.all_to_all(array, 'lm', 0, 0, tiled=True)  17.1 us
  transfers between devices with their start and end apart: 5, of which 3 were waited for; matrix products, arithmetic and copies ran while one was open for 0% of the time, Pallas kernels for 5%

profile of v6, /device:TPU:1, one launch (start us, length us, event | category | flops | bytes accessed | tf_op | source)
XLA Modules:
  0.0 94.8 jit_solution(12977736496149383287)
XLA Ops:
  1.3 2.1 %shard_map.104 = (f32[16,8,256]{2,1,0:T(8,128)}, f32[8,256]{1,0:T(8,128)}, f32[8,256]{1,0:T(8,128)}, s32[8,128]{1,0:T(8,128)}, s32[8,128]{1,0:T(8,128)}) custom-call(s32[1]{0:T(128)S(6)} %copy.11.count_ref, f32[3,512]{1,0:T(4,128)} %points_hbm.1, f32[6,1024]{1,0:T(8,128)} %poses_hbm.1, f32[6,1024]{1,0:T(8,128)} %odometry_hbm.1, f32[1,1024]{1,0:T(1,128)} %bitcast.5, ...), custom_call_target="tpu_custom_call" | custom-call | tf_op jit(solution)/shard_map/pallas_call | solution.py:488
  3.3 0.0 copy-start.2
  3.4 10.1 %all-to-all-start = ((f32[16,8,256]{2,1,0:T(8,128)}), f32[16,8,256]{2,1,0:T(8,128)S(1)}, u32[]{:S(2)}, u32[]{:S(2)}) async-start(f32[16,8,256]{2,1,0:T(8,128)} %get-tuple-element.13), calls=%async_computation | async-start | bytes 262144 | tf_op jit(solution)/shard_map/all_to_all | solution.py:499
  13.5 0.0 copy-start.3
  13.5 0.0 copy-start
  13.5 4.4 %shard_map.105.seen_ref = bf16[3,48,64,128]{3,2,1,0:T(8,128)(2,1)S(1)} custom-call(bf16[3,64,64,96]{3,2,1,0:T(8,128)(2,1)} %bitcast.4), custom_call_target="tpu_custom_call" | custom-call | tf_op jit(solution)/shard_map/pallas_call | solution.py:488
  17.9 0.0 copy-start.1
  17.9 4.8 %all-to-all-done.window_ref = f32[16,8,256]{2,1,0:T(8,128)S(1)} async-done(((f32[16,8,256]{2,1,0:T(8,128)}), f32[16,8,256]{2,1,0:T(8,128)S(1)}, u32[]{:S(2)}, u32[]{:S(2)}) %all-to-all-start) | async-done | bytes 131104 | tf_op jit(solution)/shard_map/all_to_all | solution.py:499
  22.7 0.0 copy-done.2
  22.7 7.4 %shard_map.106 = (f32[16,11,4,128]{3,2,1,0:T(4,128)}, f32[3,8,256]{2,1,0:T(8,128)S(1)}) custom-call(f32[16,8,256]{2,1,0:T(8,128)S(1)} %all-to-all-done.window_ref, s32[8,128]{1,0:T(8,128)S(1)} %copy-done.2, bf16[3,48,64,128]{3,2,1,0:T(8,128)(2,1)S(1)} %shard_map.105.seen_ref), custom_call_target="tpu_custom_call" | custom-call | tf_op jit(solution)/shard_map/pallas_call | solution.py:488
  30.1 3.5 %all-to-all-start.1 = ((f32[16,11,4,128]{3,2,1,0:T(4,128)}), f32[16,11,4,128]{3,2,1,0:T(4,128)S(1)}, u32[]{:S(2)}, u32[]{:S(2)}) async-start(f32[16,11,4,128]{3,2,1,0:T(4,128)} %get-tuple-element.15), calls=%async_computation.1 | async-start | bytes 720896 | tf_op jit(solution)/shard_map/all_to_all | solution.py:499
  33.6 0.0 copy-done.3
  33.6 0.7 collective-permute-start
  34.3 0.0 collective-permute-done.edge_hbm.first_edge_hbm
  34.3 12.6 %all-to-all-done.1.sums_ref = f32[16,11,4,128]{3,2,1,0:T(4,128)S(1)} async-done(((f32[16,11,4,128]{3,2,1,0:T(4,128)}), f32[16,11,4,128]{3,2,1,0:T(4,128)S(1)}, u32[]{:S(2)}, u32[]{:S(2)}) %all-to-all-start.1) | async-done | bytes 360480 | tf_op jit(solution)/shard_map/all_to_all | solution.py:499
  46.8 0.0 copy-done
  46.9 0.4 shard_map.107
  47.3 11.7 %all_to_all.25.window_ref = f32[16,8,256]{2,1,0:T(8,128)S(1)} all-to-all(f32[16,8,256]{2,1,0:T(8,128)S(1)} %get-tuple-element.19), channel_id=1, replica_groups=mesh['tm'=32,'lm'=16] {'lm'}, dimensions={0} | all-to-all | bytes 262144 | tf_op jit(solution)/shard_map/all_to_all | solution.py:499
  59.0 0.0 copy-done.1
  59.0 7.4 %shard_map.108 = (f32[16,11,4,128]{3,2,1,0:T(4,128)}, f32[3,8,256]{2,1,0:T(8,128)S(1)}) custom-call(f32[16,8,256]{2,1,0:T(8,128)S(1)} %all_to_all.25.window_ref, s32[8,128]{1,0:T(8,128)S(1)} %copy-done.1, bf16[3,48,64,128]{3,2,1,0:T(8,128)(2,1)S(1)} %shard_map.105.seen_ref), custom_call_target="tpu_custom_call" | custom-call | tf_op jit(solution)/shard_map/pallas_call | solution.py:488
  66.4 3.5 %all-to-all-start.3 = ((f32[16,11,4,128]{3,2,1,0:T(4,128)}), f32[16,11,4,128]{3,2,1,0:T(4,128)S(1)}, u32[]{:S(2)}, u32[]{:S(2)}) async-start(f32[16,11,4,128]{3,2,1,0:T(4,128)} %get-tuple-element.21), calls=%async_computation.3 | async-start | bytes 720896 | tf_op jit(solution)/shard_map/all_to_all | solution.py:499
  69.9 0.7 collective-permute-start.1
  70.6 0.0 collective-permute-done.1.edge_hbm
  70.6 13.0 %all-to-all-done.3.sums_ref = f32[16,11,4,128]{3,2,1,0:T(4,128)S(1)} async-done(((f32[16,11,4,128]{3,2,1,0:T(4,128)}), f32[16,11,4,128]{3,2,1,0:T(4,128)S(1)}, u32[]{:S(2)}, u32[]{:S(2)}) %all-to-all-start.3) | async-done | bytes 360480 | tf_op jit(solution)/shard_map/all_to_all | solution.py:499
  83.6 0.3 shard_map.109
  84.0 9.9 %all_to_all.26.copies_ref = f32[16,1,384]{2,1,0:T(1,128)S(1)} all-to-all(f32[16,1,384]{2,1,0:T(1,128)S(1)} %shard_map.109), channel_id=1, replica_groups=mesh['tm'=32,'lm'=16] {'lm'}, dimensions={0} | all-to-all | bytes 49152 | tf_op jit(solution)/shard_map/all_to_all | solution.py:499
  93.9 0.9 shard_map.110
Async XLA Ops:
  3.3 19.3 %copy-start.2 = (s32[8,128]{1,0:T(8,128)S(1)}, s32[8,128]{1,0:T(8,128)}, u32[]{:S(2)}) copy-start(s32[8,128]{1,0:T(8,128)} %get-tuple-element.14.names_ref) | copy-start | bytes 12292
  3.4 19.3 %all-to-all-start = ((f32[16,8,256]{2,1,0:T(8,128)}), f32[16,8,256]{2,1,0:T(8,128)S(1)}, u32[]{:S(2)}, u32[]{:S(2)}) async-start(f32[16,8,256]{2,1,0:T(8,128)} %get-tuple-element.13), calls=%async_computation | async-start | bytes 262144 | tf_op jit(solution)/shard_map/all_to_all | solution.py:499
  13.5 20.1 %copy-start.3 = (f32[8,256]{1,0:T(8,128)S(1)}, f32[8,256]{1,0:T(8,128)}, u32[]{:S(2)}) copy-start(f32[8,256]{1,0:T(8,128)} %get-tuple-element.18) | copy-start | bytes 24580
  13.5 33.3 %copy-start = (f32[8,256]{1,0:T(8,128)S(1)}, f32[8,256]{1,0:T(8,128)}, u32[]{:S(2)}) copy-start(f32[8,256]{1,0:T(8,128)} %get-tuple-element.17.link_hbm) | copy-start | bytes 24580
  17.9 41.1 %copy-start.1 = (s32[8,128]{1,0:T(8,128)S(1)}, s32[8,128]{1,0:T(8,128)}, u32[]{:S(2)}) copy-start(s32[8,128]{1,0:T(8,128)} %get-tuple-element.20.names_ref) | copy-start | bytes 12292
  30.1 16.7 %all-to-all-start.1 = ((f32[16,11,4,128]{3,2,1,0:T(4,128)}), f32[16,11,4,128]{3,2,1,0:T(4,128)S(1)}, u32[]{:S(2)}, u32[]{:S(2)}) async-start(f32[16,11,4,128]{3,2,1,0:T(4,128)} %get-tuple-element.15), calls=%async_computation.1 | async-start | bytes 720896 | tf_op jit(solution)/shard_map/all_to_all | solution.py:499
  33.6 0.7 collective-permute-start
  66.4 17.2 %all-to-all-start.3 = ((f32[16,11,4,128]{3,2,1,0:T(4,128)}), f32[16,11,4,128]{3,2,1,0:T(4,128)S(1)}, u32[]{:S(2)}, u32[]{:S(2)}) async-start(f32[16,11,4,128]{3,2,1,0:T(4,128)} %get-tuple-element.21), calls=%async_computation.3 | async-start | bytes 720896 | tf_op jit(solution)/shard_map/all_to_all | solution.py:499
  69.9 0.7 collective-permute-start.1
